TPU v7x, 32 devices: a whole 2x2x4 slice. The times are simulated.
32 devices in a mesh: wave: 8 (over z, y), lev: 4 (over x, core).
Axes of the slice: x: 2, y: 2, z: 4, core: 2. Of those that a mesh axis runs over, the one named last changes fastest.
Arguments:
- fine_state: float32 [8, 3, 2, 24, 49], P('lev', None, None, 'wave'), may hold values from -6 to 6
- fold_pairs: int32 [24], replicated, may hold values from 0 to 23, each once
- legendre: bfloat16 [24, 96, 49], P('wave', 'lev'), may hold values from -0.875 to 0.875
- gauss_weights: float32 [96], P('lev'), may hold values from 0.5 to 3
- grid_coef: float32 [8, 2560], replicated, may hold values from -4 to 4
- modes_from: float32 [8, 8], replicated
- modes_to: float32 [8, 8], replicated, as said below
- mode_rates: float32 [8], replicated, may hold values from 0.2 to 20
Outputs:
- corrected: float32 [8, 2, 2, 24, 49], P('lev', None, None, 'wave')
- fine_tend: float32 [8, 3, 2, 24, 49], P('lev', None, None, 'wave')
Inputs may be any that keep to these rules, and one draw needn't show every extreme that they name: Slot p holds zonal wavenumbers fold_pairs[p] and 47 - fold_pairs[p]; every value occurs once. modes_to is the inverse of modes_from.
All inputs are finite; a program needn't handle non-finite values.
Results may differ from a plain program's by a relative error of at most 0.02.
Values may be sent and summed in bfloat16 or wider, within the bound.
No kernel may reach another device: no remote copies, remote signals or barrier semaphores. Data moves between devices by JAX's collectives and lax.ppermute only.
A program may use at most 64 MiB of HBM per device.

v0:
```python
import math

import jax
import jax.numpy as jnp
from jax import lax
from jax.sharding import PartitionSpec as P

STEP_HALF = 0.5
quad_weights = ((5.0 / 24.0, 1.0 / 3.0, -1.0 / 24.0), (-1.0 / 24.0, 1.0 / 3.0, 5.0 / 24.0))
HIGHEST = lax.Precision.HIGHEST


def fourier_table(waves, points, amplitude):
    steps = jnp.arange(points, dtype=jnp.int32)
    turns = waves[:, :, None] * steps[None, None, :] % points
    angles = turns.astype(jnp.float32) * (2.0 * math.pi / points)
    return jnp.stack([jnp.cos(angles) * amplitude, -jnp.sin(angles) * amplitude]).astype(
        jnp.bfloat16
    )


def fine_rows(small_wave, fine_width):
    row_ids = jnp.arange(fine_width + 1, dtype=jnp.int32)[None, :]
    return row_ids < fine_width - small_wave[:, None]


def coarse_rows(small_wave, coarse):
    row_ids = jnp.arange(coarse, dtype=jnp.int32)[None, :]
    coarse_keep = row_ids < coarse - small_wave[:, None]
    degree = (small_wave[:, None] + row_ids).astype(jnp.float32)
    return (coarse_keep, degree)


def legendre_inverse(spectral, legendre_table, row_mask):
    split_spec = spectral[:, :, :, :, None, :] * row_mask[None, None, None]
    return jnp.einsum(
        "abcpmr,plr->abcpml", split_spec, legendre_table, preferred_element_type=jnp.float32
    ).astype(jnp.bfloat16)


def legendre_forward(returned, legendre_table, row_mask):
    members = jnp.einsum(
        "abcpml,plr->abcpmr", returned, legendre_table, preferred_element_type=jnp.float32
    )
    return jnp.sum(members * row_mask.astype(jnp.float32)[None, None, None], axis=4)


def grid_step(fourier, wave_table, coef, weights, factor):
    grid_field = jnp.einsum(
        "abcpmz,cpmk->abzk", fourier, wave_table, preferred_element_type=jnp.float32
    )
    product = (coef[:, None, None, :] * grid_field * grid_field).astype(jnp.bfloat16)
    returned = jnp.einsum(
        "abzk,cpmk->abcpmz", product, wave_table, preferred_element_type=jnp.float32
    )
    return (returned * (weights * factor)).astype(jnp.bfloat16)


def mix(matrix, values):
    return jnp.einsum("ql,lbcpr->qbcpr", matrix, values, precision=HIGHEST)


def per_device(
    fine_state, fold_pairs, legendre, gauss_weights, grid_coef, modes_from, modes_to, mode_rates
):
    n_wave = lax.axis_size("wave")
    wave_idx = lax.axis_index("wave")
    lev_idx = lax.axis_index("lev")
    lev_dev = fine_state.shape[0]
    pairs_dev = fine_state.shape[3]
    fine_width = fine_state.shape[4] - 1
    coarse = fine_width // 2
    longitudes = grid_coef.shape[1]
    band_size = legendre.shape[1] // n_wave
    small_wave = lax.dynamic_slice_in_dim(fold_pairs, wave_idx * pairs_dev, pairs_dev)
    first_member = fine_rows(small_wave, fine_width)
    member_mask = jnp.stack([first_member, jnp.logical_not(first_member)], 1).astype(jnp.bfloat16)
    coarse_keep, degree = coarse_rows(small_wave, coarse)
    keep_mask = coarse_keep[:, None, :].astype(jnp.bfloat16)
    keep_float = coarse_keep.astype(jnp.float32)
    fine_table = fourier_table(
        jnp.stack([fold_pairs, fine_width - 1 - fold_pairs], 1), longitudes, fine_width ** (-0.5)
    )
    coarse_table = fourier_table(fold_pairs[:, None], longitudes // 2, coarse ** (-0.5))
    coarse_leg = legendre[:, :, :coarse]
    coarse_coef = grid_coef[:, ::2]
    band_gauss = lax.dynamic_slice_in_dim(gauss_weights, wave_idx * band_size, band_size)
    local_to = lax.dynamic_slice_in_dim(modes_to, lev_idx * lev_dev, lev_dev, 1)
    local_from = lax.dynamic_slice_in_dim(modes_from, lev_idx * lev_dev, lev_dev, 1)
    mode_decay = lax.dynamic_slice_in_dim(mode_rates, lev_idx * lev_dev, lev_dev)

    def project(partial_sum):
        return mix(modes_to, partial_sum)

    def coarse_start(modes):
        gathered = lax.all_gather(modes, "lev", axis=0, tiled=True)
        levels = (mix(modes_from, gathered) * keep_float).astype(jnp.bfloat16)
        return legendre_inverse(levels, coarse_leg, keep_mask)

    def coarse_grid_step(fourier):
        return grid_step(
            fourier, coarse_table, coarse_coef, band_gauss, 2.0 * coarse / (longitudes // 2)
        )

    def coarse_finish(returned):
        partial_sum = legendre_forward(returned, coarse_leg, keep_mask)
        return lax.psum_scatter(
            project(partial_sum).astype(jnp.bfloat16), "lev", scatter_dimension=0, tiled=True
        ).astype(jnp.float32)

    def coarse_eval(modes):
        fourier = lax.all_to_all(
            coarse_start(modes), "wave", split_axis=5, concat_axis=3, tiled=True
        )
        returned = lax.all_to_all(
            coarse_grid_step(fourier), "wave", split_axis=3, concat_axis=5, tiled=True
        )
        return coarse_finish(returned)

    restricted = fine_state[..., :coarse] * keep_float
    fine_spec = lax.all_gather(fine_state.astype(jnp.bfloat16), "lev", axis=0, tiled=True)
    fine_fourier = legendre_inverse(fine_spec, legendre, member_mask)
    fine_fourier = lax.all_to_all(fine_fourier, "wave", split_axis=5, concat_axis=3, tiled=True)
    fine_back = lax.all_to_all(
        grid_step(fine_fourier, fine_table, grid_coef, band_gauss, 2.0 * fine_width / longitudes),
        "wave",
        split_axis=3,
        concat_axis=5,
        tiled=True,
    )
    fine_tend = lax.psum_scatter(
        legendre_forward(fine_back, legendre, member_mask).astype(jnp.bfloat16),
        "lev",
        scatter_dimension=0,
        tiled=True,
    ).astype(jnp.float32)
    restricted_tend = fine_tend[..., :coarse] * keep_float
    stacked = jnp.concatenate([restricted, restricted_tend], 1)
    both_modes = lax.psum_scatter(
        mix(local_to, stacked).astype(jnp.bfloat16), "lev", scatter_dimension=0, tiled=True
    ).astype(jnp.float32)
    nodes = fine_state.shape[1]
    old_state = both_modes[:, :nodes]
    old_tend = both_modes[:, nodes:]
    old_coarse = coarse_eval(old_state[:, 1:2])
    stiffness = (
        mode_decay[:, None, None, None]
        * (degree * (degree + 1.0) / (coarse * (coarse + 1.0)))[None, None]
    )
    source = old_tend - stiffness[:, None] * old_state
    integral_mid = (
        quad_weights[0][0] * source[:, 0]
        + quad_weights[0][1] * source[:, 1]
        + quad_weights[0][2] * source[:, 2]
    )
    integral_end = (
        quad_weights[1][0] * source[:, 0]
        + quad_weights[1][1] * source[:, 1]
        + quad_weights[1][2] * source[:, 2]
    )
    divisor = 1.0 + STEP_HALF * stiffness
    next_mid = (old_state[:, 0] + STEP_HALF * stiffness * old_state[:, 1] + integral_mid) / divisor
    coarse_fresh = coarse_eval(next_mid[:, None])
    next_end = (
        next_mid
        + STEP_HALF * (coarse_fresh[:, 0] - old_coarse[:, 0])
        + STEP_HALF * stiffness * old_state[:, 2]
        + integral_end
    ) / divisor
    change = jnp.stack([next_mid - old_state[:, 1], next_end - old_state[:, 2]], 1)
    lifted = lax.psum_scatter(
        mix(local_from, change).astype(jnp.bfloat16), "lev", scatter_dimension=0, tiled=True
    ).astype(jnp.float32)
    corrected = fine_state[:, 1:] + jnp.pad(
        lifted, ((0, 0), (0, 0), (0, 0), (0, 0), (0, fine_width + 1 - coarse))
    )
    return (corrected, fine_tend)


def solution(mesh):
    placed = (
        P("lev", None, None, "wave", None),
        P(),
        P("wave", "lev", None),
        P("lev"),
        P(),
        P(),
        P(),
        P(),
    )
    return jax.shard_map(
        per_device,
        mesh=mesh,
        in_specs=placed,
        out_specs=(P("lev", None, None, "wave", None), P("lev", None, None, "wave", None)),
        check_vma=False,
    )
```

profile of v0, /device:TPU:0, one launch (start us, length us, event | category | flops | bytes accessed | tf_op | source)
XLA Modules:
  0.0 130.4 jit_solution(1549815140402897033)
XLA Ops:
  0.6 0.0 copy-start
  0.7 0.7 broadcast_subtract_fusion.1
  1.4 0.1 iota_compare_fusion.1
  1.5 6.2 %all_gather.9 = bf16[8,3,2,3,49]{4,2,3,1,0:T(2,128)(2,1)S(1)} all-gather(bf16[2,3,2,3,49]{4,2,3,1,0:T(2,128)(2,1)S(1)} %convert_element_type.212), channel_id=1, replica_groups=mesh['wave'=8,'lev'=4] {'lev'}, dimensions={0}, use_global_device_ids=true | all-gather | bytes 17640 | tf_op jit(solution)/shard_map/all_gather | solution.py:121
  7.7 0.7 copy-done.1
  8.4 0.1 fusion.2
  8.6 0.2 copy.95
  8.7 0.8 reshape.468
  9.6 6.4 %all-to-all-start = ((bf16[8,2,432]{2,1,0:T(2,128)(2,1)}), bf16[8,2,432]{2,1,0:T(2,128)(2,1)S(1)}, u32[]{:S(2)}, u32[]{:S(2)}) async-start(bf16[8,2,432]{2,1,0:T(2,128)(2,1)} %reshape.468), calls=%async_computation | async-start | bytes 32768 | tf_op jit(solution)/shard_map/all_to_all | solution.py:123
  16.0 0.1 fusion.97
  16.1 0.6 multiply_convert_fusion.3
  16.7 2.3 %multiply_convert_fusion.1 = (bf16[1,24,2,2560]{3,1,2,0:T(8,128)(2,1)S(1)}, bf16[1,24,2,2560]{3,1,2,0:T(8,128)(2,1)S(1)}) fusion(s32[24,2]{0,1:T(2,128)S(1)} %pad_add_fusion), kind=kLoop, calls=%fused_computation.52 | loop fusion | flops 1720320 | bytes 491712 | tf_op jit(solution)/shard_map/convert.4
  19.1 0.6 copy-done.6
  19.7 0.1 dynamic_slice.19
  19.8 0.1 broadcast_multiply_fusion
  19.9 0.6 copy-done.7
  20.4 0.1 dynamic-slice_multiply_fusion
  20.5 2.1 %all-to-all-done = bf16[8,2,432]{2,1,0:T(2,128)(2,1)S(1)} async-done(((bf16[8,2,432]{2,1,0:T(2,128)(2,1)}), bf16[8,2,432]{2,1,0:T(2,128)(2,1)S(1)}, u32[]{:S(2)}, u32[]{:S(2)}) %all-to-all-start) | async-done | bytes 13856 | tf_op jit(solution)/shard_map/all_to_all | solution.py:123
  22.6 0.2 reshape.469
  22.8 0.2 copy.97
  23.0 0.7 copy-done.3
  23.7 0.8 fusion.3
  24.6 0.2 copy.99
  24.7 0.8 reshape.470
  25.6 3.9 %all-to-all-start.1 = ((bf16[8,2,432]{2,1,0:T(2,128)(2,1)}), bf16[8,2,432]{2,1,0:T(2,128)(2,1)S(1)}, u32[]{:S(2)}, u32[]{:S(2)}) async-start(bf16[8,2,432]{2,1,0:T(2,128)(2,1)} %reshape.470), calls=%async_computation.1 | async-start | bytes 32768 | tf_op jit(solution)/shard_map/all_to_all | solution.py:124
  29.5 0.1 fusion.110
  29.5 1.4 %slice.58 = f32[8,1280]{1,0:T(8,128)S(1)} slice(f32[8,2560]{1,0:T(8,128)S(1)} %copy-done.3), slice={[0:8:1], [0:2560:2]} | slice | bytes 81920 | tf_op jit(solution)/shard_map/slice | solution.py:86
  31.0 0.6 copy-done.8
  31.6 0.6 dynamic-slice
  32.9 3.2 %all-to-all-done.1 = bf16[8,2,432]{2,1,0:T(2,128)(2,1)S(1)} async-done(((bf16[8,2,432]{2,1,0:T(2,128)(2,1)}), bf16[8,2,432]{2,1,0:T(2,128)(2,1)S(1)}, u32[]{:S(2)}, u32[]{:S(2)}) %all-to-all-start.1) | async-done | bytes 13856 | tf_op jit(solution)/shard_map/all_to_all | solution.py:124
  36.0 0.2 reshape.471
  36.3 0.2 copy.101
  36.4 0.2 fusion
  36.7 10.5 %all-reduce.1 = bf16[8,3,2,3,49]{4,0,3,2,1:T(8,128)(2,1)S(1)} all-reduce(bf16[8,3,2,3,49]{4,0,3,2,1:T(8,128)(2,1)S(1)} %copy.103), channel_id=2, replica_groups=mesh['wave'=8,'lev'=4] {'lev'}, use_global_device_ids=true, to_apply=%region_1.2.clone | all-reduce | flops 7056 | bytes 28224
  47.2 0.3 convolution_convert_fusion
  47.6 11.7 %all-reduce.2 = bf16[8,6,2,3,24]{4,0,3,2,1:T(8,128)(2,1)S(1)} all-reduce(bf16[8,6,2,3,24]{4,0,3,2,1:T(8,128)(2,1)S(1)} %convolution_convert_fusion), channel_id=3, replica_groups=mesh['wave'=8,'lev'=4] {'lev'}, use_global_device_ids=true, to_apply=%region_2.3.clone | all-reduce | flops 6912 | bytes 27648
  59.4 5.2 %all_gather.10 = f32[8,1,2,3,24]{4,2,3,1,0:T(2,128)S(1)} all-gather(f32[2,1,2,3,24]{4,2,3,1,0:T(2,128)S(1)} %copy.104), channel_id=1, replica_groups=mesh['wave'=8,'lev'=4] {'lev'}, dimensions={0}, use_global_device_ids=true | all-gather | bytes 5760 | tf_op jit(solution)/shard_map/all_gather | solution.py:96
  64.6 0.2 fusion.23
  64.8 0.1 fusion.14
  64.9 0.7 copy.106
  65.6 3.3 %all-to-all-start.2 = ((bf16[8,1,2,3,1,24]{0,2,3,4,1,5:T(2,128)(2,1)}), bf16[8,1,2,3,1,24]{0,2,3,4,1,5:T(2,128)(2,1)S(1)}, u32[]{:S(2)}, u32[]{:S(2)}) async-start(bf16[8,1,2,3,1,24]{0,2,3,4,1,5:T(2,128)(2,1)} %copy.106), calls=%async_computation.2 | async-start | bytes 73728 | tf_op jit(solution)/shard_map/all_to_all | solution.py:112
  69.0 5.2 %all_gather.11 = f32[8,1,2,3,24]{4,2,3,1,0:T(2,128)S(1)} all-gather(f32[2,1,2,3,24]{4,2,3,1,0:T(2,128)S(1)} %copy.114), channel_id=1, replica_groups=mesh['wave'=8,'lev'=4] {'lev'}, dimensions={0}, use_global_device_ids=true | all-gather | bytes 5760 | tf_op jit(solution)/shard_map/all_gather | solution.py:96
  74.2 0.2 fusion.20
  74.4 0.1 fusion.16
  74.5 0.6 copy.125
  75.1 0.7 copy.116
  75.8 5.9 %all-to-all-start.4 = ((bf16[8,1,2,3,1,24]{0,2,3,4,1,5:T(2,128)(2,1)}), bf16[8,1,2,3,1,24]{0,2,3,4,1,5:T(2,128)(2,1)S(1)}, u32[]{:S(2)}, u32[]{:S(2)}) async-start(bf16[8,1,2,3,1,24]{0,2,3,4,1,5:T(2,128)(2,1)} %copy.116), calls=%async_computation.4 | async-start | bytes 73728 | tf_op jit(solution)/shard_map/all_to_all | solution.py:112
  81.8 0.4 fusion.21
  82.2 0.8 copy.110
  82.9 5.5 %all-to-all-done.4 = bf16[8,1,2,3,1,24]{0,2,3,4,1,5:T(2,128)(2,1)S(1)} async-done(((bf16[8,1,2,3,1,24]{0,2,3,4,1,5:T(2,128)(2,1)}), bf16[8,1,2,3,1,24]{0,2,3,4,1,5:T(2,128)(2,1)S(1)}, u32[]{:S(2)}, u32[]{:S(2)}) %all-to-all-start.4) | async-done | bytes 2336 | tf_op jit(solution)/shard_map/all_to_all | solution.py:112
  88.4 3.3 %all-to-all-start.3 = ((bf16[8,1,2,24,1,3]{0,2,5,4,1,3:T(2,128)(2,1)}), bf16[8,1,2,24,1,3]{0,2,5,4,1,3:T(2,128)(2,1)S(1)}, u32[]{:S(2)}, u32[]{:S(2)}) async-start(bf16[8,1,2,24,1,3]{0,2,5,4,1,3:T(2,128)(2,1)} %copy.110), calls=%async_computation.3 | async-start | bytes 73728 | tf_op jit(solution)/shard_map/all_to_all | solution.py:115
  91.9 0.4 fusion.18
  92.2 0.7 copy.120
  93.0 5.5 %all-to-all-done.3 = bf16[8,1,2,24,1,3]{0,2,5,4,1,3:T(2,128)(2,1)S(1)} async-done(((bf16[8,1,2,24,1,3]{0,2,5,4,1,3:T(2,128)(2,1)}), bf16[8,1,2,24,1,3]{0,2,5,4,1,3:T(2,128)(2,1)S(1)}, u32[]{:S(2)}, u32[]{:S(2)}) %all-to-all-start.3) | async-done | bytes 2336 | tf_op jit(solution)/shard_map/all_to_all | solution.py:115
  98.4 3.3 %all-to-all-start.5 = ((bf16[8,1,2,24,1,3]{0,2,5,4,1,3:T(2,128)(2,1)}), bf16[8,1,2,24,1,3]{0,2,5,4,1,3:T(2,128)(2,1)S(1)}, u32[]{:S(2)}, u32[]{:S(2)}) async-start(bf16[8,1,2,24,1,3]{0,2,5,4,1,3:T(2,128)(2,1)} %copy.120), calls=%async_computation.5 | async-start | bytes 73728 | tf_op jit(solution)/shard_map/all_to_all | solution.py:115
  101.8 0.2 fusion.7
  102.0 0.2 fusion.15
  102.2 6.2 %all-to-all-done.5 = bf16[8,1,2,24,1,3]{0,2,5,4,1,3:T(2,128)(2,1)S(1)} async-done(((bf16[8,1,2,24,1,3]{0,2,5,4,1,3:T(2,128)(2,1)}), bf16[8,1,2,24,1,3]{0,2,5,4,1,3:T(2,128)(2,1)S(1)}, u32[]{:S(2)}, u32[]{:S(2)}) %all-to-all-start.5) | async-done | bytes 2336 | tf_op jit(solution)/shard_map/all_to_all | solution.py:115
  108.5 0.2 fusion.9
  108.7 0.2 fusion.17
  108.8 10.3 %all-reduce.6 = (bf16[8,1,2,3,24]{4,0,3,2,1:T(8,128)(2,1)S(1)}, bf16[8,1,2,3,24]{4,0,3,2,1:T(8,128)(2,1)S(1)}) all-reduce(bf16[8,1,2,3,24]{4,0,3,2,1:T(8,128)(2,1)S(1)} %fusion.17, bf16[8,1,2,3,24]{4,0,3,2,1:T(8,128)(2,1)S(1)} %fusion.15), channel_id=5, replica_groups=mesh['wave'=8,'lev'=4] {'lev'}, use_global_device_ids=true, to_apply=%region_4.5.clone | all-reduce | flops 2304 | bytes 9216
  119.1 0.2 convolution_convert_fusion.2
  119.4 10.4 %all-reduce.5 = bf16[8,2,2,3,24]{4,0,3,2,1:T(8,128)(2,1)S(1)} all-reduce(bf16[8,2,2,3,24]{4,0,3,2,1:T(8,128)(2,1)S(1)} %convolution_convert_fusion.2), channel_id=6, replica_groups=mesh['wave'=8,'lev'=4] {'lev'}, use_global_device_ids=true, to_apply=%region_5.6.clone | all-reduce | flops 2304 | bytes 9216
  129.8 0.6 copy.124
  (37 shorter events, 0.4 us)
Async XLA Ops:
  0.6 46.6 %copy-start = (f32[8,8]{1,0:T(8,128)S(1)}, f32[8,8]{1,0:T(8,128)}, u32[]{:S(2)}) copy-start(f32[8,8]{1,0:T(8,128)} %param.14) | copy-start | bytes 772
  0.6 0.8 copy-start.2
  7.7 0.7 copy-start.1
  9.6 6.4 %copy-start.5 = (s32[24]{0:T(128)S(1)}, s32[24]{0:T(128)}, u32[]{:S(2)}) copy-start(s32[24]{0:T(128)} %param.9) | copy-start | bytes 292
  9.6 13.0 %all-to-all-start = ((bf16[8,2,432]{2,1,0:T(2,128)(2,1)}), bf16[8,2,432]{2,1,0:T(2,128)(2,1)S(1)}, u32[]{:S(2)}, u32[]{:S(2)}) async-start(bf16[8,2,432]{2,1,0:T(2,128)(2,1)} %reshape.468), calls=%async_computation | async-start | bytes 32768 | tf_op jit(solution)/shard_map/all_to_all | solution.py:123
  19.0 0.7 copy-start.6
  19.8 0.7 copy-start.7
  22.8 0.9 copy-start.3
  25.6 10.5 %all-to-all-start.1 = ((bf16[8,2,432]{2,1,0:T(2,128)(2,1)}), bf16[8,2,432]{2,1,0:T(2,128)(2,1)S(1)}, u32[]{:S(2)}, u32[]{:S(2)}) async-start(bf16[8,2,432]{2,1,0:T(2,128)(2,1)} %reshape.470), calls=%async_computation.1 | async-start | bytes 32768 | tf_op jit(solution)/shard_map/all_to_all | solution.py:124
  31.0 0.7 copy-start.8
  59.3 5.3 %copy-start.4 = (f32[8,8]{1,0:T(8,128)S(1)}, f32[8,8]{1,0:T(8,128)}, u32[]{:S(2)}) copy-start(f32[8,8]{1,0:T(8,128)} %param.13) | copy-start | bytes 772
  65.6 10.2 %all-to-all-start.2 = ((bf16[8,1,2,3,1,24]{0,2,3,4,1,5:T(2,128)(2,1)}), bf16[8,1,2,3,1,24]{0,2,3,4,1,5:T(2,128)(2,1)S(1)}, u32[]{:S(2)}, u32[]{:S(2)}) async-start(bf16[8,1,2,3,1,24]{0,2,3,4,1,5:T(2,128)(2,1)} %copy.106), calls=%async_computation.2 | async-start | bytes 73728 | tf_op jit(solution)/shard_map/all_to_all | solution.py:112
  75.8 12.6 %all-to-all-start.4 = ((bf16[8,1,2,3,1,24]{0,2,3,4,1,5:T(2,128)(2,1)}), bf16[8,1,2,3,1,24]{0,2,3,4,1,5:T(2,128)(2,1)S(1)}, u32[]{:S(2)}, u32[]{:S(2)}) async-start(bf16[8,1,2,3,1,24]{0,2,3,4,1,5:T(2,128)(2,1)} %copy.116), calls=%async_computation.4 | async-start | bytes 73728 | tf_op jit(solution)/shard_map/all_to_all | solution.py:112
  88.4 10.0 %all-to-all-start.3 = ((bf16[8,1,2,24,1,3]{0,2,5,4,1,3:T(2,128)(2,1)}), bf16[8,1,2,24,1,3]{0,2,5,4,1,3:T(2,128)(2,1)S(1)}, u32[]{:S(2)}, u32[]{:S(2)}) async-start(bf16[8,1,2,24,1,3]{0,2,5,4,1,3:T(2,128)(2,1)} %copy.110), calls=%async_computation.3 | async-start | bytes 73728 | tf_op jit(solution)/shard_map/all_to_all | solution.py:115
  98.4 10.0 %all-to-all-start.5 = ((bf16[8,1,2,24,1,3]{0,2,5,4,1,3:T(2,128)(2,1)}), bf16[8,1,2,24,1,3]{0,2,5,4,1,3:T(2,128)(2,1)S(1)}, u32[]{:S(2)}, u32[]{:S(2)}) async-start(bf16[8,1,2,24,1,3]{0,2,5,4,1,3:T(2,128)(2,1)} %copy.120), calls=%async_computation.5 | async-start | bytes 73728 | tf_op jit(solution)/shard_map/all_to_all | solution.py:115
where the time goes:
time: 131 us; the launch traced here: 130 us
  blocking collectives  59.5 us (45%)
  starting transfers between devices  26.3 us (20%)
  waiting for transfers between devices  22.5 us (17%)
  local copies, waits for them, and re-layouts  12.5 us (10%)
  other arithmetic  4.17 us (3%)
  matrix products  3.8 us (3%)
  between operations  1.69 us (1%)
    unnamed x4, blocking collectives  42.8 us
    all_to_all x2, waiting for transfers between devices, coarse_eval(): lax.all_to_all(coarse_grid_step(fourier), 'wave', split_axis=3, concat_ax...  11.7 us
    all_gather x2, blocking collectives, coarse_start(): gathered = lax.all_gather(modes, 'lev', axis=0, tiled=True)  10.4 us
    all_to_all x2, starting transfers between devices, coarse_eval(): lax.all_to_all(coarse_start(modes), 'wave', split_axis=5, concat_axis=3,...  9.25 us
    unnamed x26, local copies, waits for them, and re-layouts  7.27 us
    all_to_all x2, starting transfers between devices, coarse_eval(): lax.all_to_all(coarse_grid_step(fourier), 'wave', split_axis=3, concat_ax...  6.68 us
    all_to_all x1, starting transfers between devices, per_device(): lax.all_to_all(fine_fourier, 'wave', split_axis=5, concat_axis=3, tiled=T...  6.43 us
    all_gather x1, blocking collectives, per_device(): lax.all_gather(fine_state.astype(jnp.bfloat16), 'lev', axis=0, tiled=True)  6.21 us
  transfers between devices with their start and end apart: 6, of which 5 were waited for; matrix products, arithmetic and copies ran while one was open for 7% of the time, Pallas kernels for 0%

commit v1 on v0

--- a/solution.py
+++ b/solution.py
@@ -1,8 +1,12 @@
+import functools
 import math
 
 import jax
 import jax.numpy as jnp
+import numpy as np
 from jax import lax
+from jax.experimental import pallas as pl
+from jax.experimental.pallas import tpu as pltpu
 from jax.sharding import PartitionSpec as P
 
 STEP_HALF = 0.5
@@ -60,7 +64,7 @@
     return jnp.einsum("ql,lbcpr->qbcpr", matrix, values, precision=HIGHEST)
 
 
-def per_device(
+def split_plan(
     fine_state, fold_pairs, legendre, gauss_weights, grid_coef, modes_from, modes_to, mode_rates
 ):
     n_wave = lax.axis_size("wave")
@@ -177,6 +181,428 @@
     return (corrected, fine_tend)
 
 
+LANES = 128
+REPLICATED_BYTES = 16 * 2**20
+
+
+def round_up(value, unit):
+    return -(-value // unit) * unit
+
+
+def interpolation(points, targets, degree):
+    offset = (
+        2.0 * np.pi * (np.arange(targets)[:, None] / targets - np.arange(points)[None, :] / points)
+    )
+    order = np.arange(1, degree + 1)
+    return (1.0 + 2.0 * np.cos(offset[:, :, None] * order).sum(-1)) / points
+
+
+def wave_rows(waves, points, amplitude):
+    turns = np.arange(waves)[:, None] * np.arange(points)[None, :] % points
+    angles = turns * (2.0 * np.pi / points)
+    return np.concatenate([np.cos(angles), -np.sin(angles)]) * amplitude
+
+
+def rows_of(column_waves, valid, waves):
+    hot = (column_waves[:, None] == jnp.arange(waves)[None, :]) & valid[:, None]
+    zero = jnp.zeros_like(hot)
+    return jnp.concatenate(
+        [jnp.concatenate([hot, zero], 1), jnp.concatenate([zero, hot], 1)]
+    ).astype(jnp.bfloat16)
+
+
+def matmul(a, b):
+    return jnp.dot(a, b, preferred_element_type=jnp.float32)
+
+
+def matmul_nt(a, b):
+    return lax.dot_general(a, b, (((1,), (1,)), ((), ())), preferred_element_type=jnp.float32)
+
+
+def matmul_exact(a, b):
+    return jnp.dot(a, b, preferred_element_type=jnp.float32, precision=lax.Precision.HIGHEST)
+
+
+def sweep_kernel(
+    size,
+    place_ref,
+    fold_ref,
+    own_ref,
+    other_ref,
+    wave_ref,
+    quad_ref,
+    coarse_wave_ref,
+    coarse_quad_ref,
+    mix_to_ref,
+    mix_from_ref,
+    mix_back_ref,
+    lift_ref,
+    rate_ref,
+    tend_ref,
+    lifted_ref,
+    leg_s,
+    state_s,
+    fourier_s,
+    back_s,
+    tend_s,
+    coarse_s,
+    coarse_back_s,
+    change_s,
+):
+    (n_wave, n_pair, lev_dev, nodes, slots, fine_width, coarse, lats) = size
+    n_lev = 2 * n_pair
+    levels = n_lev * lev_dev
+    dev_rows = lev_dev * nodes * 2
+    rows = levels * nodes * 2
+    all_lats = n_lev * lats
+    wide = leg_s.shape[2]
+    fine_columns = n_wave * slots * 2
+    coarse_columns = n_wave * slots
+    lane = lax.broadcasted_iota(jnp.int32, (1, wide), 1)
+    head = slots * coarse
+    rest = fine_width + 1 - coarse
+    lane_slot = jnp.full((1, wide), -1, jnp.int32)
+    lane_row = jnp.zeros((1, wide), jnp.int32)
+    for s in range(slots):
+        inside = (lane >= s * coarse) & (lane < (s + 1) * coarse)
+        lane_slot = jnp.where(inside, s, lane_slot)
+        lane_row = jnp.where(inside, lane - s * coarse, lane_row)
+        begin = head + s * rest
+        inside = (lane >= begin) & (lane < begin + rest)
+        lane_slot = jnp.where(inside, s, lane_slot)
+        lane_row = jnp.where(inside, lane - begin + coarse, lane_row)
+
+    def lane_wave(w):
+        value = jnp.zeros((1, wide), jnp.int32)
+        for s in range(slots):
+            value = jnp.where(lane_slot == s, fold_ref[w * slots + s], value)
+        return value
+
+    member_masks, slot_masks, keeps, stiffs = [], [], [], []
+    for w in range(n_wave):
+        small = lane_wave(w)
+        first = lane_row < fine_width - small
+        masks = []
+        for s in range(slots):
+            own_slot = lane_slot == s
+            masks.append((own_slot & first).astype(jnp.float32))
+            masks.append((own_slot & jnp.logical_not(first)).astype(jnp.float32))
+        member_masks.append(masks)
+        in_coarse = (lane < head) & (lane_row < coarse - small)
+        keep = in_coarse[:, :LANES].astype(jnp.float32)
+        keeps.append(keep)
+        slot_masks.append([keep * (lane_slot[:, :LANES] == s).astype(jnp.float32) for s in range(slots)])
+        degree = (small + lane_row)[:, :LANES].astype(jnp.float32)
+        stiffs.append(rate_ref[...] * (degree * (degree + 1.0) / (coarse * (coarse + 1.0))))
+
+    weights_lane = slots * (fine_width + 1)
+    for w in range(n_wave):
+        for x in range(n_pair):
+            for o, ref in enumerate((own_ref, other_ref)):
+                d = 2 * x + o
+                block = ref[w * n_pair + x].astype(jnp.float32)
+                leg_s[w, d * lats : (d + 1) * lats, :] = block[:lats]
+                state_s[w, d * dev_rows : (d + 1) * dev_rows, :] = block[lats : lats + dev_rows]
+        if all_lats < leg_s.shape[1]:
+            leg_s[w, all_lats:, :] = jnp.zeros((leg_s.shape[1] - all_lats, wide), jnp.float32)
+
+    def legendre(w):
+        return leg_s[w].astype(jnp.bfloat16)
+
+    def weighted(w):
+        table = leg_s[w]
+        column = table[:, weights_lane : weights_lane + 1] + table[:, weights_lane + 1 : weights_lane + 2]
+        return (table * column).astype(jnp.bfloat16)
+
+    for w in range(n_wave):
+        state = state_s[w]
+        left = jnp.concatenate([state * mask for mask in member_masks[w]], 0).astype(jnp.bfloat16)
+        out = matmul_nt(left, legendre(w))
+        for j in range(2 * slots):
+            fourier_s[pl.ds(w * 2 * slots + j, rows, stride=fine_columns), :] = out[j * rows : (j + 1) * rows]
+
+    both = 2 * fine_columns
+    for a in range(levels):
+        pieces = [
+            fourier_s[(a * nodes + b) * both : (a * nodes + b + 1) * both, :].astype(jnp.bfloat16)
+            for b in range(nodes)
+        ]
+        grid = matmul(wave_ref[...], jnp.concatenate(pieces, 1))
+        product = (grid * grid).astype(jnp.bfloat16)
+        back = matmul(quad_ref[a], product)
+        for b in range(nodes):
+            back_s[(a * nodes + b) * both : (a * nodes + b + 1) * both, :] = back[:, b * LANES : (b + 1) * LANES]
+
+    stacked = []
+    for w in range(n_wave):
+        left = jnp.concatenate(
+            [
+                back_s[pl.ds(w * 2 * slots + j, rows, stride=fine_columns), :].astype(jnp.bfloat16)
+                for j in range(2 * slots)
+            ],
+            0,
+        )
+        out = matmul(left, weighted(w))
+        total = member_masks[w][0] * out[:rows]
+        for j in range(1, 2 * slots):
+            total = total + member_masks[w][j] * out[j * rows : (j + 1) * rows]
+        tend_s[w] = total
+        stacked.append(state_s[w][:, :LANES] * keeps[w])
+        stacked.append(total[:, :LANES] * keeps[w])
+    place = place_ref[0]
+    begin = pl.multiple_of(place_ref[1] * (2 * dev_rows), 8)
+    tend_ref[...] = tend_s[place, pl.ds(begin, dev_rows), :]
+
+    modes = matmul_exact(mix_to_ref[...], jnp.concatenate(stacked, 1))
+    per_node = levels * 2
+    evals, later, old_of, mid_of = [], [], [], []
+    for w in range(n_wave):
+        old, source = [], []
+        stiff = stiffs[w]
+        for b in range(nodes):
+            part = modes[b * per_node : (b + 1) * per_node]
+            old.append(part[:, 2 * w * LANES : (2 * w + 1) * LANES])
+            source.append(part[:, (2 * w + 1) * LANES : (2 * w + 2) * LANES] - stiff * old[-1])
+        divisor = 1.0 + STEP_HALF * stiff
+        mid = sum(quad_weights[0][b] * source[b] for b in range(nodes))
+        mid = (mid + old[0] + STEP_HALF * stiff * old[1]) / divisor
+        end = sum(quad_weights[1][b] * source[b] for b in range(nodes))
+        end = end + mid + STEP_HALF * stiff * old[2]
+        evals.append(old[1])
+        evals.append(mid)
+        later.append((end, divisor))
+        old_of.append(old)
+        mid_of.append(mid)
+
+    level_values = matmul_exact(mix_from_ref[...], jnp.concatenate(evals, 1))
+    for w in range(n_wave):
+        left = jnp.concatenate(
+            [
+                level_values[:, (2 * w + e) * LANES : (2 * w + e + 1) * LANES] * slot_masks[w][s]
+                for s in range(slots)
+                for e in range(2)
+            ],
+            0,
+        ).astype(jnp.bfloat16)
+        out = matmul_nt(left, legendre(w)[:, :LANES])
+        for s in range(slots):
+            for e in range(2):
+                at = (s * 2 + e) * per_node
+                coarse_s[e, pl.ds(w * slots + s, per_node, stride=coarse_columns), :] = out[at : at + per_node]
+
+    both_c = 2 * coarse_columns
+    for a in range(levels):
+        pieces = [coarse_s[e, a * both_c : (a + 1) * both_c, :].astype(jnp.bfloat16) for e in range(2)]
+        grid = matmul(coarse_wave_ref[...], jnp.concatenate(pieces, 1))
+        product = (grid * grid).astype(jnp.bfloat16)
+        back = matmul(coarse_quad_ref[a], product)
+        for e in range(2):
+            coarse_back_s[e, a * both_c : (a + 1) * both_c, :] = back[:, e * LANES : (e + 1) * LANES]
+
+    tends = []
+    for w in range(n_wave):
+        left = jnp.concatenate(
+            [
+                coarse_back_s[e, pl.ds(w * slots + s, per_node, stride=coarse_columns), :].astype(jnp.bfloat16)
+                for s in range(slots)
+                for e in range(2)
+            ],
+            0,
+        )
+        out = matmul(left, weighted(w)[:, :LANES])
+        for e in range(2):
+            total = None
+            for s in range(slots):
+                at = (s * 2 + e) * per_node
+                term = slot_masks[w][s] * out[at : at + per_node]
+                total = term if total is None else total + term
+            tends.append(total)
+    coarse_modes = matmul_exact(mix_back_ref[...], jnp.concatenate(tends, 1))
+    for w in range(n_wave):
+        before = coarse_modes[:, 2 * w * LANES : (2 * w + 1) * LANES]
+        fresh = coarse_modes[:, (2 * w + 1) * LANES : (2 * w + 2) * LANES]
+        end, divisor = later[w]
+        end = (end + STEP_HALF * (fresh - before)) / divisor
+        change_s[w, :per_node, :] = mid_of[w] - old_of[w][1]
+        change_s[w, per_node:, :] = end - old_of[w][2]
+    lifted_ref[...] = matmul_exact(lift_ref[...], change_s[place])
+
+
+def replicated_plan(
+    fine_state, fold_pairs, legendre, gauss_weights, grid_coef, modes_from, modes_to, mode_rates
+):
+    n_wave = lax.axis_size("wave")
+    n_lev = lax.axis_size("lev")
+    wave_idx = lax.axis_index("wave")
+    lev_idx = lax.axis_index("lev")
+    n_pair = n_lev // 2
+    core = lev_idx % 2
+    lev_dev, nodes, _, slots, fine_rows_count = fine_state.shape
+    fine_width = fine_rows_count - 1
+    coarse = fine_width // 2
+    lats = legendre.shape[1]
+    levels = lev_dev * n_lev
+    longitudes = grid_coef.shape[1]
+    head, rest = slots * coarse, slots * (fine_rows_count - coarse)
+    dev_rows = lev_dev * nodes * 2
+    wide = round_up(head + rest + 2, LANES)
+    block_rows = round_up(lats + dev_rows, 8)
+    bf = jnp.bfloat16
+
+    def lanes_first(values):
+        flat = values.shape[:-2]
+        return [
+            values[..., :coarse].reshape(flat + (head,)),
+            values[..., coarse:].reshape(flat + (rest,)),
+        ]
+
+    weight_high = gauss_weights.astype(bf)
+    weight_low = (gauss_weights - weight_high.astype(jnp.float32)).astype(bf)
+    table = jnp.concatenate(
+        lanes_first(jnp.swapaxes(legendre, 0, 1)) + [weight_high[:, None], weight_low[:, None]], 1
+    )
+    state = jnp.concatenate(lanes_first(fine_state.astype(bf).reshape(dev_rows, slots, fine_rows_count)), 1)
+    block = jnp.concatenate(
+        [
+            jnp.pad(table, ((0, 0), (0, wide - table.shape[1]))),
+            jnp.pad(state, ((0, block_rows - lats - dev_rows), (0, wide - state.shape[1]))),
+        ]
+    )
+    chips = n_wave * n_pair
+    groups = [[2 * i + c for i in range(chips)] for c in range(2)]
+    own = lax.all_to_all(
+        jnp.broadcast_to(block[None], (chips,) + block.shape),
+        ("wave", "lev"),
+        0,
+        0,
+        tiled=True,
+        axis_index_groups=groups,
+    )
+    other = lax.ppermute(own, ("wave", "lev"), [(i, i ^ 1) for i in range(2 * chips)])
+
+    points = round_up(4 * (fine_width - 1) + 1, 32)
+    coarse_points = round_up(4 * (coarse - 1) + 1, 32)
+    fine_amp, coarse_amp = fine_width**-0.5, coarse**-0.5
+    small = fold_pairs.reshape(n_wave * slots)
+    column_waves = jnp.stack([small, fine_width - 1 - small], 1).reshape(-1)
+    hot = rows_of(column_waves, column_waves >= 0, fine_width)
+    coarse_hot = rows_of(small, small >= 0, coarse)
+
+    def by_level(values):
+        paired = values.reshape(n_pair, 2, lev_dev, -1)
+        return jnp.where(core == 1, paired[:, ::-1], paired).reshape(values.shape)
+
+    coef = by_level(grid_coef)
+
+    def tables(waves, amplitude, count, degree, stride, one_hot, factor):
+        sampled = jnp.asarray(wave_rows(waves, count, amplitude).T, bf)
+        basis = np.zeros((2 * waves, longitudes))
+        basis[:, ::stride] = wave_rows(waves, longitudes // stride, amplitude * factor)
+        spread = interpolation(count, longitudes, degree)
+        scaled = (coef[:, None, :] * jnp.asarray(basis, jnp.float32)[None]).astype(bf)
+        quad = jnp.einsum(
+            "amk,kj->amj", scaled, jnp.asarray(spread, bf), preferred_element_type=jnp.float32
+        ).astype(bf)
+        synth = jnp.einsum("jm,cm->jc", sampled, one_hot, preferred_element_type=jnp.float32).astype(bf)
+        quad = jnp.einsum("cm,amj->acj", one_hot, quad, preferred_element_type=jnp.float32).astype(bf)
+        return synth, quad
+
+    wave_table, quad_table = tables(
+        fine_width, fine_amp, points, 2 * (fine_width - 1), 1, hot, 2.0 * fine_width / longitudes
+    )
+    coarse_wave, coarse_quad = tables(
+        coarse, coarse_amp, coarse_points, 2 * (coarse - 1), 2, coarse_hot, 2.0 * coarse / (longitudes // 2)
+    )
+
+    to_rows = by_level(modes_to.T).T
+    from_rows = by_level(modes_from)
+    eye_c, eye_b = jnp.eye(2, dtype=jnp.float32), jnp.eye(nodes, dtype=jnp.float32)
+    mix_to = jnp.einsum("qa,bd,ce->bqcade", to_rows, eye_b, eye_c).transpose(0, 1, 2, 3, 4, 5)
+    mix_to = mix_to.reshape(nodes * levels * 2, levels * nodes * 2)
+    mix_from = jnp.einsum("aq,ce->acqe", from_rows, eye_c).reshape(levels * 2, levels * 2)
+    mix_back = jnp.einsum("qa,ce->qcae", to_rows, eye_c).reshape(levels * 2, levels * 2)
+    own_from = lax.dynamic_slice_in_dim(modes_from, lev_idx * lev_dev, lev_dev, 0)
+    lift = jnp.einsum("aq,bd,ce->abcdqe", own_from, jnp.eye(nodes - 1, dtype=jnp.float32), eye_c)
+    lift = lift.reshape(lev_dev * (nodes - 1) * 2, (nodes - 1) * levels * 2)
+    rates = jnp.broadcast_to(jnp.repeat(mode_rates, 2)[:, None], (levels * 2, LANES))
+    place = jnp.stack([wave_idx, lev_idx // 2]).astype(jnp.int32)
+
+    size = (n_wave, n_pair, lev_dev, nodes, slots, fine_width, coarse, lats)
+    vmem = pl.BlockSpec(memory_space=pltpu.VMEM)
+    smem = pl.BlockSpec(memory_space=pltpu.SMEM)
+    rows = levels * nodes * 2
+    lat_rows = round_up(n_lev * lats, LANES)
+    f32 = jnp.float32
+    tend, lifted = pl.pallas_call(
+        functools.partial(sweep_kernel, size),
+        out_shape=(
+            jax.ShapeDtypeStruct((dev_rows, wide), f32),
+            jax.ShapeDtypeStruct((lev_dev * (nodes - 1) * 2, LANES), f32),
+        ),
+        in_specs=[smem, smem] + [vmem] * 11,
+        out_specs=(vmem, vmem),
+        scratch_shapes=[
+            pltpu.VMEM((n_wave, lat_rows, wide), f32),
+            pltpu.VMEM((n_wave, rows, wide), f32),
+            pltpu.VMEM((rows * n_wave * slots * 2, lat_rows), f32),
+            pltpu.VMEM((rows * n_wave * slots * 2, lat_rows), f32),
+            pltpu.VMEM((n_wave, rows, wide), f32),
+            pltpu.VMEM((2, levels * 2 * n_wave * slots, lat_rows), f32),
+            pltpu.VMEM((2, levels * 2 * n_wave * slots, lat_rows), f32),
+            pltpu.VMEM((n_wave, (nodes - 1) * levels * 2, LANES), f32),
+        ],
+        name="sweep",
+    )(
+        place,
+        fold_pairs,
+        own,
+        other,
+        wave_table,
+        quad_table,
+        coarse_wave,
+        coarse_quad,
+        mix_to,
+        mix_from,
+        mix_back,
+        lift,
+        rates,
+    )
+
+    def slots_last(values, width):
+        return values.reshape(values.shape[0], slots, width)
+
+    fine_tend = jnp.concatenate(
+        [
+            slots_last(tend[:, :head], coarse),
+            slots_last(tend[:, head : head + rest], fine_rows_count - coarse),
+        ],
+        2,
+    ).reshape(fine_state.shape)
+    raised = lifted[:, :head].reshape(lev_dev, nodes - 1, 2, slots, coarse)
+    corrected = fine_state[:, 1:] + jnp.pad(
+        raised, ((0, 0), (0, 0), (0, 0), (0, 0), (0, fine_rows_count - coarse))
+    )
+    return (corrected, fine_tend)
+
+
+def fits_replicated(fine_state, legendre):
+    n_wave, n_lev = lax.axis_size("wave"), lax.axis_size("lev")
+    slots, fine_rows_count = fine_state.shape[3:]
+    gathered = 4 * n_wave * n_lev * (legendre.size + fine_state.size)
+    return (
+        n_lev % 2 == 0
+        and slots * (fine_rows_count // 2) <= LANES
+        and n_lev * legendre.shape[1] <= LANES
+        and fine_state.shape[1] == len(quad_weights[0])
+        and gathered * 8 <= REPLICATED_BYTES
+    )
+
+
+def per_device(fine_state, fold_pairs, legendre, *rest):
+    plan = replicated_plan if fits_replicated(fine_state, legendre) else split_plan
+    return plan(fine_state, fold_pairs, legendre, *rest)
+
+
 def solution(mesh):
     placed = (
         P("lev", None, None, "wave", None),

time: 131 us -> 39.9 us (0.30)
  blocking collectives: 59.5 us -> 0 us
  waiting for transfers between devices: 22.5 us -> 1.73 us
  starting transfers between devices: 26.3 us -> 8.48 us
  Pallas kernels: 0 us -> 7.38 us
  matrix products: 3.8 us -> 6.08 us
    unnamed x4 -> x0, blocking collectives: 42.8 us -> none
    all_to_all x6 -> x1, waiting for transfers between devices: 22.5 us -> 1.73 us  [replicated_plan(): lax.all_to_all(jnp.broadcast_to(block[None], (chips,) + block.shape), ('w...]
    all_to_all x6 -> x1, starting transfers between devices: 26.3 us -> 8.47 us  [replicated_plan(): lax.all_to_all(jnp.broadcast_to(block[None], (chips,) + block.shape), ('w...]
    all_gather x3 -> x0, blocking collectives: 16.6 us -> none  [the longest x2 10.4 us: coarse_start(): gathered = lax.all_gather(modes, 'lev', axis=0, tiled=True)]
    pallas_call x0 -> x1, Pallas kernels: none -> 7.38 us  [replicated_plan(): pl.pallas_call(functools.partial(sweep_kernel, size), out_shape=(jax.Shap...]
    unnamed x26 -> x25, local copies, waits for them, and re-layouts: 7.27 us -> 1.35 us
    reshape x0 -> x12, local copies, waits for them, and re-layouts: none -> 4.13 us  [the longest x2 0.9 us: replicated_plan(): mix_to = mix_to.reshape(nodes * levels * 2, levels * nodes * 2)]
    convert_element_type x7 -> x2, local copies, waits for them, and re-layouts: 3.26 us -> 0.71 us  [the longest x1 0.7 us: tables(): jnp.einsum('jm,cm->jc', sampled, one_hot, preferred_element_type=jnp.floa...]
  transfers between devices with their start and end apart: 6 -> 2, of which waited for: 5 -> 1; matrix products, arithmetic and copies ran while one was open for 7% -> 30% of each run, Pallas kernels for 0% -> 0%
where the time goes in v1:
time: 39.9 us; the launch traced here: 39.3 us
  local copies, waits for them, and re-layouts  11.7 us (29%)
  starting transfers between devices  8.48 us (21%)
  Pallas kernels  7.38 us (18%)
  matrix products  6.08 us (15%)
  other arithmetic  3.04 us (8%)
  waiting for transfers between devices  1.73 us (4%)
  between operations  0.89 us (2%)
    all_to_all x1, starting transfers between devices, replicated_plan(): lax.all_to_all(jnp.broadcast_to(block[None], (chips,) + block.shape), ('w...  8.47 us
    pallas_call x1, Pallas kernels, replicated_plan(): pl.pallas_call(functools.partial(sweep_kernel, size), out_shape=(jax.Shap...  7.38 us
    dot_general x2, matrix products, tables(): jnp.einsum('cm,amj->acj', one_hot, quad, preferred_element_type=jnp.float32)  5.07 us
    all_to_all x1, waiting for transfers between devices, replicated_plan(): lax.all_to_all(jnp.broadcast_to(block[None], (chips,) + block.shape), ('w...  1.73 us
    unnamed x25, local copies, waits for them, and re-layouts  1.35 us
    dot_general x2, matrix products, tables(): jnp.einsum('jm,cm->jc', sampled, one_hot, preferred_element_type=jnp.floa...  1.01 us
    slice x4, local copies, waits for them, and re-layouts, lanes_first(): values[..., coarse:].reshape(flat + (rest,))  0.94 us
    reshape x2, local copies, waits for them, and re-layouts, replicated_plan(): mix_to = mix_to.reshape(nodes * levels * 2, levels * nodes * 2)  0.9 us
  transfers between devices with their start and end apart: 2, of which 1 were waited for; matrix products, arithmetic and copies ran while one was open for 30% of the time, Pallas kernels for 0%

profile of v1, /device:TPU:0, one launch (start us, length us, event | category | flops | bytes accessed | tf_op | source)
XLA Modules:
  0.0 39.3 jit_solution(6589329080950571011)
XLA Ops:
  0.6 0.0 copy-start.6
  0.6 0.0 copy-start.2
  0.7 0.0 copy-start.7
  0.7 0.0 copy-start.5
  0.7 0.8 %slice.33 = bf16[24,3,25]{2,0,1:T(8,128)(2,1)S(1)} slice(bf16[24,3,49]{2,0,1:T(8,128)(2,1)} %bitcast.62), slice={[0:24], [0:3], [24:49]} | slice | bytes 7200 | tf_op jit(solution)/shard_map/slice | solution.py:456
  1.5 0.1 reshape.71
  1.6 0.7 %copy.47 = bf16[24,3,24]{2,1,0:T(4,128)(2,1)S(1)} copy(bf16[24,3,24]{2,0,1:T(8,128)(2,1)} %bitcast.63) | data formatting | bytes 6912 | tf_op jit(solution)/shard_map/slice | solution.py:455
  2.4 0.1 reshape.70
  2.4 0.7 %convert_bitcast_fusion.1 = (bf16[24,1]{0,1:T(2,128)(2,1)S(1)}, bf16[24,1]{0,1:T(2,128)(2,1)S(1)}) fusion(f32[24]{0:T(128)} %param.17), kind=kLoop, calls=%fused_computation.61 | loop fusion | flops 96 | bytes 192 | tf_op jit(solution)/shard_map/broadcast_in_dim | solution.py:462
  3.2 0.1 copy.49
  3.3 0.1 copy.50
  3.4 0.7 %convert_element_type.58 = bf16[2,3,2,3,49]{4,2,3,1,0:T(2,128)(2,1)S(1)} convert(f32[2,3,2,3,49]{4,2,3,1,0:T(2,128)} %param.14) | non-fusion elementwise | flops 1764 | bytes 10584 | tf_op jit(solution)/shard_map/convert_element_type | solution.py:464
  4.2 0.1 slice.35
  4.2 0.1 reshape.74
  4.3 0.1 reshape.73
  4.4 0.1 fusion.29
  4.5 0.1 fusion.27
  4.6 0.7 %broadcast_in_dim.14 = bf16[16,40,256]{2,1,0:T(8,128)(2,1)} broadcast(bf16[40,256]{1,0:T(8,128)(2,1)S(1)} %pad_maximum_fusion.1), dimensions={1,2} | broadcast | bytes 348160 | tf_op jit(solution)/shard_map/broadcast_in_dim | solution.py:474
  5.4 8.5 %all-to-all-start = ((bf16[16,40,256]{2,1,0:T(8,128)(2,1)}), bf16[16,40,256]{2,1,0:T(8,128)(2,1)S(1)}, u32[]{:S(2)}, u32[]{:S(2)}) async-start(bf16[16,40,256]{2,1,0:T(8,128)(2,1)} %broadcast_in_dim.14), calls=%async_computation | async-start | bytes 655360 | tf_op jit(solution)/shard_map/all_to_all | solution.py:473
  13.9 0.0 copy-done.6
  13.9 0.1 copy.59
  14.0 0.1 broadcast_multiply_fusion.1
  14.1 0.1 reshape.75
  14.2 0.1 copy.54
  14.2 0.1 eq.48
  14.3 0.0 copy-done.7
  14.4 0.1 copy.60
  14.5 0.0 copy-done.5
  14.5 0.1 copy.61
  14.6 0.1 broadcast_multiply_fusion
  14.6 0.1 multiply_bitcast_fusion
  14.7 0.1 fusion.28
  14.8 0.1 multiply_bitcast_fusion.2
  14.9 0.1 multiply_bitcast_fusion.1
  15.0 0.2 convolution_convert_fusion.2
  15.2 0.1 fusion.18
  15.3 0.1 mul.31
  15.3 0.2 reshape.78
  15.6 0.7 %copy.62.mix_to_ref = f32[48,48]{1,0:T(8,128)} copy(f32[48,48]{0,1:T(8,128)S(1)} %reshape.78) | data formatting | bytes 18432 | tf_op jit(solution)/shard_map/reshape | solution.py:521
  16.3 0.7 %reshape.81.mix_from_ref = f32[16,16]{1,0:T(8,128)} reshape(f32[8,2,8,2]{3,2,1,0:T(8,128)S(1)} %get-tuple-element.11) | data formatting | bytes 2048 | tf_op jit(solution)/shard_map/reshape | solution.py:522
  16.9 0.7 %reshape.82.mix_back_ref = f32[16,16]{1,0:T(8,128)} reshape(f32[8,2,8,2]{3,2,1,0:T(8,128)S(1)} %get-tuple-element.10) | data formatting | bytes 2048 | tf_op jit(solution)/shard_map/reshape | solution.py:523
  17.6 0.7 %reshape.83.lift_ref = f32[8,32]{1,0:T(8,128)} reshape(f32[2,2,2,2,8,2]{5,4,3,2,1,0:T(8,128)S(1)} %multiply_bitcast_fusion.1) | data formatting | bytes 2048 | tf_op jit(solution)/shard_map/reshape | solution.py:526
  18.3 0.7 %copy.58 = bf16[48,96]{0,1:T(8,128)(2,1)} copy(bf16[48,96]{1,0:T(8,128)(2,1)S(1)} %convolution_convert_fusion.2) | data formatting | bytes 18432 | tf_op jit(solution)/shard_map/convert_element_type | solution.py:506
  19.0 0.1 broadcast_in_dim.15
  19.1 0.1 broadcast_in_dim.16
  19.1 0.7 %pad_add_fusion.7.place_ref = s32[2]{0:T(128)} fusion(s32[1]{0:T(128)} %bitcast.1, s32[1]{0:T(128)} %bitcast), kind=kLoop, calls=%fused_computation.58 | loop fusion | flops 2 | bytes 16 | tf_op jit(solution)/shard_map/stack | solution.py:528
  19.8 0.8 %fusion.12.wave_ref = bf16[192,96]{1,0:T(8,128)(2,1)} fusion(bf16[192,96]{1,0:T(8,128)(2,1)S(1)} %copy-done.3, pred[48,48]{1,0:T(8,128)(4,1)S(1)} %fusion.18), kind=kOutput, calls=%fused_computation.16 | convolution fusion | flops 3566592 | bytes 76032 | tf_op jit(solution)/shard_map/jm,cm->jc/dot_general | solution.py:506
  20.7 2.8 %fusion.11.coarse_quad_ref = bf16[8,48,96]{2,1,0:T(8,128)(2,1)} fusion(bf16[2560,96,1]{0,1,2:T(8,128)(2,1)} %constant.83, f32[48,2560]{1,0:T(8,128)} %constant.64.clone, f32[8,2560]{1,0:T(8,128)S(1)} %mul.31, pred[24,24]{1,0:T(8,128)(4,1)S(1)} %fusion.28), kind=kOutput, calls=%fused_computation.14 | convolution fusion | flops 194324736 | bytes 1139264 | tf_op jit(solution)/shard_map/cm,amj->acj/dot_general | solution.py:507
  23.4 1.7 %all-to-all-done.own_ref = bf16[16,40,256]{2,1,0:T(8,128)(2,1)S(1)} async-done(((bf16[16,40,256]{2,1,0:T(8,128)(2,1)}), bf16[16,40,256]{2,1,0:T(8,128)(2,1)S(1)}, u32[]{:S(2)}, u32[]{:S(2)}) %all-to-all-start) | async-done | bytes 327712 | tf_op jit(solution)/shard_map/all_to_all | solution.py:473
  25.2 0.0 collective-permute-start
  25.2 0.0 copy-done.9
  25.2 0.0 copy-done.10
  25.2 2.3 %fusion.9.quad_ref = bf16[8,96,192]{2,1,0:T(8,128)(2,1)} fusion(bf16[2560,192,1]{0,1,2:T(8,128)(2,1)S(1)} %copy-done.10, f32[96,2560]{1,0:T(8,128)S(1)} %copy-done.9, f32[8,2560]{1,0:T(8,128)S(1)} %mul.31, pred[48,48]{1,0:T(8,128)(4,1)S(1)} %fusion.18), kind=kOutput, calls=%fused_computation.11 | convolution fusion | flops 787522560 | bytes 2345216 | tf_op jit(solution)/shard_map/cm,amj->acj/dot_general | solution.py:507
  27.5 0.0 collective-permute-done.other_ref
  27.5 0.7 %broadcast_in_dim.17.rate_ref = f32[16,128]{1,0:T(8,128)} broadcast(f32[16]{0:T(128)S(1)} %broadcast_in_dim.16), dimensions={0} | broadcast | bytes 8256 | tf_op jit(solution)/shard_map/broadcast_in_dim | solution.py:527
  28.2 7.4 %sweep.1 = (f32[12,256]{1,0:T(8,128)}, f32[8,128]{1,0:T(8,128)}) custom-call(s32[2]{0:T(128)} %pad_add_fusion.7.place_ref, s32[24]{0:T(128)} %fold_ref.1, bf16[16,40,256]{2,1,0:T(8,128)(2,1)} %copy-done, bf16[16,40,256]{2,1,0:T(8,128)(2,1)} %copy-done.1, bf16[192,96]{1,0:T(8,128)(2,1)} %fusion.12.wave_ref, bf16[8,96,192]{2,1,0:T(8,128)(2,1)} %fusion.9.quad_ref, ...), custom_call_target="tpu_custom_call" | custom-call | tf_op jit(solution)/shard_map/sweep/pallas_call | solution.py:536
  35.6 0.7 %slice.30 = f32[12,72]{1,0:T(8,128)S(1)} slice(f32[12,256]{1,0:T(8,128)} %get-tuple-element.5), slice={[0:12], [0:72]} | slice | bytes 6912 | tf_op jit(solution)/shard_map/slice | solution.py:576
  36.3 0.8 %slice.31 = f32[12,75]{1,0:T(8,128)S(1)} slice(f32[12,256]{1,0:T(8,128)} %get-tuple-element.5), slice={[0:12], [72:147]} | slice | bytes 7200 | tf_op jit(solution)/shard_map/slice | solution.py:577
  37.1 0.1 concatenate.44
  37.2 0.1 concatenate.45
  37.3 0.1 pad_maximum_fusion
  37.3 0.6 %copy.64 = f32[2,3,2,3,49]{4,2,3,1,0:T(2,128)} copy(f32[2,3,2,3,49]{4,3,2,1,0:T(4,128)S(1)} %pad_maximum_fusion) | data formatting | bytes 14112
  38.0 0.8 %reshape.84 = f32[2,2,2,3,24]{4,3,2,1,0:T(4,128)S(1)} reshape(f32[8,72]{1,0:T(8,128)} %bitcast.70) | data formatting | bytes 4608 | tf_op jit(solution)/shard_map/reshape | solution.py:581
  38.7 0.6 %copy.63 = f32[2,2,2,3,49]{4,2,3,1,0:T(2,128)} copy(f32[2,2,2,3,49]{4,3,2,1,0:T(4,128)S(1)} %copy_add_fusion) | data formatting | bytes 9408
  (31 shorter events, 0.2 us)
Async XLA Ops:
  0.6 13.2 %copy-start.6 = (s32[24]{0:T(128)S(1)}, s32[24]{0:T(128)}, u32[]{:S(2)}) copy-start(s32[24]{0:T(128)} %fold_ref.1) | copy-start | bytes 292
  0.6 13.4 %copy-start.2 = (f32[8,2560]{1,0:T(8,128)S(1)}, f32[8,2560]{1,0:T(8,128)}, u32[]{:S(2)}) copy-start(f32[8,2560]{1,0:T(8,128)} %param.18) | copy-start | bytes 245764
  0.7 13.7 %copy-start.7 = (f32[8,8]{1,0:T(8,128)S(1)}, f32[8,8]{1,0:T(8,128)}, u32[]{:S(2)}) copy-start(f32[8,8]{1,0:T(8,128)} %param.20) | copy-start | bytes 772
  0.7 13.8 %copy-start.5 = (f32[8,8]{1,0:T(8,128)S(1)}, f32[8,8]{1,0:T(8,128)}, u32[]{:S(2)}) copy-start(f32[8,8]{1,0:T(8,128)} %param.19) | copy-start | bytes 772
  5.4 9.6 %copy-start.4 = (bf16[96,48]{1,0:T(8,128)(2,1)S(1)}, bf16[96,48]{1,0:T(8,128)(2,1)}, u32[]{:S(2)}) copy-start(bf16[96,48]{1,0:T(8,128)(2,1)} %constant.63.clone) | copy-start | bytes 27652
  5.4 19.8 %all-to-all-start = ((bf16[16,40,256]{2,1,0:T(8,128)(2,1)}), bf16[16,40,256]{2,1,0:T(8,128)(2,1)S(1)}, u32[]{:S(2)}, u32[]{:S(2)}) async-start(bf16[16,40,256]{2,1,0:T(8,128)(2,1)} %broadcast_in_dim.14), calls=%async_computation | async-start | bytes 655360 | tf_op jit(solution)/shard_map/all_to_all | solution.py:473
  14.6 4.4 %copy-start.8 = (f32[8]{0:T(128)S(1)}, f32[8]{0:T(128)}, u32[]{:S(2)}) copy-start(f32[8]{0:T(128)} %param.21) | copy-start | bytes 100
  14.6 5.2 %copy-start.3 = (bf16[192,96]{1,0:T(8,128)(2,1)S(1)}, bf16[192,96]{1,0:T(8,128)(2,1)}, u32[]{:S(2)}) copy-start(bf16[192,96]{1,0:T(8,128)(2,1)} %constant.60.clone) | copy-start | bytes 110596
  20.7 4.5 %copy-start.9 = (f32[96,2560]{1,0:T(8,128)S(1)}, f32[96,2560]{1,0:T(8,128)}, u32[]{:S(2)}) copy-start(f32[96,2560]{1,0:T(8,128)} %constant.61.clone) | copy-start | bytes 2949124
  20.7 4.5 %copy-start.10 = (bf16[2560,192,1]{0,1,2:T(8,128)(2,1)S(1)}, bf16[2560,192,1]{0,1,2:T(8,128)(2,1)}, u32[]{:S(2)}) copy-start(bf16[2560,192,1]{0,1,2:T(8,128)(2,1)} %constant.82) | copy-start | bytes 2949124
  25.2 2.3 %copy-start = (bf16[16,40,256]{2,1,0:T(8,128)(2,1)}, bf16[16,40,256]{2,1,0:T(8,128)(2,1)S(1)}, u32[]{:S(2)}) copy-start(bf16[16,40,256]{2,1,0:T(8,128)(2,1)S(1)} %all-to-all-done.own_ref) | copy-start | bytes 983044
  25.2 2.3 %collective-permute-start = (bf16[16,40,256]{2,1,0:T(8,128)(2,1)S(1)}, bf16[16,40,256]{2,1,0:T(8,128)(2,1)S(1)}, u32[]{:S(2)}, u32[]{:S(2)}) collective-permute-start(bf16[16,40,256]{2,1,0:T(8,128)(2,1)S(1)} %all-to-all-done.own_ref), channel_id=1, source_target_pairs={{0,1},{1,0},{2,3},{3,2},{4,5},{5,4},{6,7},{7,6},{8,9},{9,8},{10,11... | collective-permute-start | bytes 983048 | tf_op jit(solution)/shard_map/ppermute | solution.py:481
  27.5 11.2 %slice-start = ((f32[2,3,2,3,49]{4,2,3,1,0:T(2,128)}), f32[2,2,2,3,49]{4,2,3,1,0:T(2,128)S(1)}, s32[]{:S(2)}) async-start(f32[2,3,2,3,49]{4,2,3,1,0:T(2,128)} %param.14), calls=%async_computation.1 | async-start | bytes 24576 | tf_op jit(solution)/shard_map/slice | solution.py:582
  27.5 0.7 %copy-start.1 = (bf16[16,40,256]{2,1,0:T(8,128)(2,1)}, bf16[16,40,256]{2,1,0:T(8,128)(2,1)S(1)}, u32[]{:S(2)}) copy-start(bf16[16,40,256]{2,1,0:T(8,128)(2,1)S(1)} %collective-permute-done.other_ref) | copy-start | bytes 983044

commit v2 on v0

--- a/solution.py
+++ b/solution.py
@@ -1,8 +1,12 @@
+import functools
 import math
 
 import jax
 import jax.numpy as jnp
+import numpy as np
 from jax import lax
+from jax.experimental import pallas as pl
+from jax.experimental.pallas import tpu as pltpu
 from jax.sharding import PartitionSpec as P
 
 STEP_HALF = 0.5
@@ -60,7 +64,7 @@
     return jnp.einsum("ql,lbcpr->qbcpr", matrix, values, precision=HIGHEST)
 
 
-def per_device(
+def split_plan(
     fine_state, fold_pairs, legendre, gauss_weights, grid_coef, modes_from, modes_to, mode_rates
 ):
     n_wave = lax.axis_size("wave")
@@ -177,6 +181,587 @@
     return (corrected, fine_tend)
 
 
+LANES = 128
+SUBLANES = 8
+REPLICATED_BYTES = 16 * 2**20
+
+
+def round_up(value, unit):
+    return -(-value // unit) * unit
+
+
+def interpolation(points, targets, degree):
+    offset = (
+        2.0 * np.pi * (np.arange(targets)[:, None] / targets - np.arange(points)[None, :] / points)
+    )
+    order = np.arange(1, degree + 1)
+    return (1.0 + 2.0 * np.cos(offset[:, :, None] * order).sum(-1)) / points
+
+
+def wave_rows(waves, points, amplitude):
+    turns = np.arange(waves)[:, None] * np.arange(points)[None, :] % points
+    angles = turns * (2.0 * np.pi / points)
+    return np.concatenate([np.cos(angles), -np.sin(angles)]) * amplitude
+
+
+def matmul(a, b):
+    return jnp.dot(a, b, preferred_element_type=jnp.float32)
+
+
+def matmul_nt(a, b):
+    return lax.dot_general(a, b, (((1,), (1,)), ((), ())), preferred_element_type=jnp.float32)
+
+
+def matmul_exact(a, b):
+    return jnp.dot(a, b, preferred_element_type=jnp.float32, precision=lax.Precision.HIGHEST)
+
+
+def high_low(values):
+    high = values.astype(jnp.bfloat16)
+    return high, (values - high.astype(jnp.float32)).astype(jnp.bfloat16)
+
+
+def matmul_split(left, right):
+    high, low = high_low(right)
+    return matmul(left, jnp.concatenate([high, low, high], 0))
+
+
+class Sizes:
+    def __init__(self, fine_state, legendre):
+        self.n_wave, self.n_lev = lax.axis_size("wave"), lax.axis_size("lev")
+        self.lev_dev, self.nodes, _, self.slots, self.fine_rows = fine_state.shape
+        self.lats = legendre.shape[1]
+        self.n_pair = self.n_lev // 2
+        self.fine_width = self.fine_rows - 1
+        self.coarse = self.fine_width // 2
+        self.levels = self.n_lev * self.lev_dev
+        self.dev_rows = self.lev_dev * self.nodes * 2
+        self.rows = self.levels * self.nodes * 2
+        self.per_node = self.levels * 2
+        self.head = self.slots * self.coarse
+        self.rest = self.fine_rows - self.coarse
+        self.used = self.slots * self.fine_rows
+        self.state_rows = round_up(self.dev_rows, SUBLANES)
+        self.groups = (self.lats + self.state_rows) // SUBLANES
+        self.unit = LANES // self.groups
+        self.block_rows = self.lats + SUBLANES + self.state_rows
+        self.chips = self.n_wave * self.n_pair
+        self.fine_columns = self.n_wave * self.slots * 2
+        self.coarse_columns = self.n_wave * self.slots
+        self.points = round_up(4 * (self.fine_width - 1) + 1, 32)
+        self.coarse_points = round_up(4 * (self.coarse - 1) + 1, 32)
+
+
+def pack_kernel(z, state_ref, leg_ref, gauss_ref, out_ref, rows_s):
+    bf, f32 = jnp.bfloat16, jnp.float32
+    row = lax.broadcasted_iota(jnp.int32, (z.fine_rows, LANES), 0)
+    lane = lax.broadcasted_iota(jnp.int32, (z.fine_rows, LANES), 1)
+    for n in range(z.dev_rows):
+        a, b, c = n // (z.nodes * 2), n // 2 % z.nodes, n % 2
+        values = state_ref[a, b, c]
+        for s in range(z.slots):
+            rows_s[s, n : n + 1, :] = values[s : s + 1]
+    if z.state_rows > z.dev_rows:
+        for s in range(z.slots):
+            rows_s[s, z.dev_rows :, :] = jnp.zeros((z.state_rows - z.dev_rows, z.fine_rows), f32)
+    table = jnp.zeros((z.lats, LANES), f32)
+    state = jnp.zeros((z.state_rows, LANES), f32)
+    extra = jnp.zeros((SUBLANES, LANES), f32)
+    for s in range(z.slots):
+        target = jnp.where(row < z.coarse, s * z.coarse + row, z.head + s * z.rest + row - z.coarse)
+        leg = leg_ref[s].astype(f32)
+        spec = rows_s[s]
+        place = (target == lane).astype(bf)
+        table = table + matmul(leg.astype(bf), place)
+        state = state + matmul(spec.astype(bf), place)
+        if z.head + (s + 1) * z.rest > LANES:
+            for q in range(z.groups):
+                at = q * SUBLANES
+                part = leg[at : at + SUBLANES] if at < z.lats else spec[at - z.lats : at - z.lats + SUBLANES]
+                place = ((target >= LANES) & (target - LANES + q * z.unit == lane)).astype(bf)
+                extra = extra + matmul(part.astype(bf), place)
+    wide_row = lax.broadcasted_iota(jnp.int32, (SUBLANES, z.lats), 0)
+    wide_lane = lax.broadcasted_iota(jnp.int32, (SUBLANES, z.lats), 1)
+    out_lane = lax.broadcasted_iota(jnp.int32, (SUBLANES, LANES), 1)
+    for q in range(z.lats // SUBLANES):
+        chosen = jnp.where(wide_lane == wide_row + q * SUBLANES, gauss_ref[...], 0.0)
+        column = jnp.sum(chosen, axis=1, keepdims=True)
+        high = column.astype(bf).astype(f32)
+        at = q * z.unit + z.used - LANES
+        extra = extra + jnp.where(out_lane == at, high, 0.0)
+        extra = extra + jnp.where(out_lane == at + 1, column - high, 0.0)
+    block = jnp.concatenate([table, extra, state], 0).astype(bf)
+    for i in range(z.chips):
+        out_ref[i] = block
+
+
+def mix_matrix(pick_left, matrix, pick_right, mask, cut):
+    values = matmul_exact(matmul_exact(pick_left, matrix), pick_right) * mask
+    high, low = high_low(values)
+    lane = lax.broadcasted_iota(jnp.int32, values.shape, 1)
+    return jnp.where(lane < cut, high.astype(jnp.float32), low.astype(jnp.float32)).astype(jnp.bfloat16)
+
+
+def tables_kernel(
+    z,
+    rate_ref,
+    fold_smem,
+    fold_ref,
+    coef_ref,
+    to_ref,
+    from_ref,
+    basis_ref,
+    spread_ref,
+    coarse_spread_ref,
+    sampled_ref,
+    coarse_sampled_ref,
+    to_left_ref,
+    to_right_ref,
+    to_mask_ref,
+    from_left_ref,
+    from_right_ref,
+    from_mask_ref,
+    back_left_ref,
+    back_right_ref,
+    lift_left_ref,
+    lift_right_ref,
+    lift_mask_ref,
+    wave_ref,
+    quad_ref,
+    coarse_wave_ref,
+    coarse_quad_ref,
+    mix_to_ref,
+    mix_from_ref,
+    mix_back_ref,
+    lift_ref,
+    member_ref,
+    slot_ref,
+    keep_ref,
+    stiff_ref,
+):
+    bf, f32 = jnp.bfloat16, jnp.float32
+    lev = lax.axis_index("lev")
+    core = lax.rem(lev, 2)
+    waves, coarse = z.fine_width, z.coarse
+    half = z.fine_columns
+
+    def wave_column(count, per_slot):
+        row = lax.broadcasted_iota(jnp.int32, (count, z.coarse_columns), 0)
+        lane = lax.broadcasted_iota(jnp.int32, (count, z.coarse_columns), 1)
+        inside = (row >= lane * per_slot) & (row < (lane + 1) * per_slot)
+        small = jnp.sum(jnp.where(inside, fold_ref[...].astype(f32), 0.0), axis=1, keepdims=True)
+        if per_slot == 1:
+            return small
+        first = lax.broadcasted_iota(jnp.int32, (count, 1), 0) & 1
+        return jnp.where(first == 0, small, waves - 1 - small)
+
+    def one_hot(count, per_slot, width):
+        column = wave_column(count, per_slot)
+        lane = lax.broadcasted_iota(jnp.int32, (count, 2 * width), 1).astype(f32)
+        top = (lane == column).astype(f32)
+        bottom = (lane == column + width).astype(f32)
+        return jnp.concatenate([top, bottom], 0).astype(bf)
+
+    hot = one_hot(half, 2, waves)
+    coarse_hot = one_hot(z.coarse_columns, 1, coarse)
+    wave_ref[...] = matmul_nt(sampled_ref[...], hot).astype(bf)
+    coarse_wave_ref[...] = matmul_nt(coarse_sampled_ref[...], coarse_hot).astype(bf)
+    for x in range(z.n_pair):
+        for o in range(2):
+            for al in range(z.lev_dev):
+                a = (2 * x + o) * z.lev_dev + al
+                level = (2 * x + (core if o == 0 else 1 - core)) * z.lev_dev + al
+                scaled = coef_ref[pl.ds(level, 1), :] * basis_ref[...].astype(f32)
+                low = jnp.concatenate([scaled[:coarse], scaled[waves : waves + coarse]], 0)
+                quad = matmul(scaled.astype(bf), spread_ref[...]).astype(bf)
+                quad_ref[a] = matmul(hot, quad).astype(bf)
+                quad = matmul(low.astype(bf), coarse_spread_ref[...]).astype(bf)
+                coarse_quad_ref[a] = matmul(coarse_hot, quad).astype(bf)
+
+    def mix(left, matrix_ref, right, mask_ref):
+        return mix_matrix(left, matrix_ref[...], right, mask_ref[...], right.shape[1] // 3 * 2)
+
+    mix_to_ref[...] = mix(to_left_ref[...], to_ref, to_right_ref[core], to_mask_ref)
+    mix_from_ref[...] = mix(from_left_ref[core], from_ref, from_right_ref[...], from_mask_ref)
+    mix_back_ref[...] = mix(back_left_ref[...], to_ref, back_right_ref[core], from_mask_ref)
+    lift_ref[...] = mix(lift_left_ref[lev], from_ref, lift_right_ref[...], lift_mask_ref)
+
+    wide = 2 * LANES
+    lane = lax.broadcasted_iota(jnp.int32, (1, wide), 1)
+    lane_slot = jnp.full((1, wide), -1, jnp.int32)
+    lane_row = jnp.zeros((1, wide), jnp.int32)
+    for s in range(z.slots):
+        for begin, width, first in ((s * coarse, coarse, 0), (z.head + s * z.rest, z.rest, coarse)):
+            inside = (lane >= begin) & (lane < begin + width)
+            lane_slot = jnp.where(inside, s, lane_slot)
+            lane_row = jnp.where(inside, lane - begin + first, lane_row)
+    rate_row = lax.broadcasted_iota(jnp.int32, (z.per_node, LANES), 0)
+    rates = jnp.zeros((z.per_node, LANES), f32)
+    for q in range(z.levels):
+        rates = jnp.where((rate_row >= 2 * q) & (rate_row < 2 * q + 2), rate_ref[q], rates)
+    for w in range(z.n_wave):
+        small = jnp.zeros((1, wide), jnp.int32)
+        for s in range(z.slots):
+            small = jnp.where(lane_slot == s, fold_smem[w * z.slots + s], small)
+        first = lane_row < waves - small
+        keep = (lane < z.head) & (lane_row < coarse - small)
+        keep_ref[w : w + 1, :] = keep[:, :LANES].astype(f32)
+        for s in range(z.slots):
+            own = lane_slot == s
+            at = (w * z.slots + s) * 2
+            member_ref[at : at + 1, :] = (own & first).astype(f32)
+            member_ref[at + 1 : at + 2, :] = (own & jnp.logical_not(first)).astype(f32)
+            slot_ref[w * z.slots + s : w * z.slots + s + 1, :] = (own & keep)[:, :LANES].astype(f32)
+        degree = (small + lane_row)[:, :LANES].astype(f32)
+        stiff_ref[w] = rates * (degree * (degree + 1.0) / (coarse * (coarse + 1.0)))
+
+
+def sweep_kernel(
+    z,
+    own_ref,
+    other_ref,
+    state_ref,
+    wave_ref,
+    quad_ref,
+    coarse_wave_ref,
+    coarse_quad_ref,
+    mix_to_ref,
+    mix_from_ref,
+    mix_back_ref,
+    lift_ref,
+    member_ref,
+    slot_ref,
+    keep_ref,
+    stiff_ref,
+    corrected_ref,
+    tend_ref,
+    leg_s,
+    state_s,
+    fourier_s,
+    back_s,
+    tend_s,
+    coarse_s,
+    coarse_back_s,
+    change_s,
+):
+    bf, f32 = jnp.bfloat16, jnp.float32
+    slots, rows, lats, per_node = z.slots, z.rows, z.lats, z.per_node
+    wide = 2 * LANES
+    all_lats = z.n_lev * lats
+
+    def member(w, j):
+        at = w * slots * 2 + j
+        return member_ref[at : at + 1, :]
+
+    def slot(w, s):
+        return slot_ref[w * slots + s : w * slots + s + 1, :]
+
+    def keep(w):
+        return keep_ref[w : w + 1, :]
+
+    for w in range(z.n_wave):
+        for x in range(z.n_pair):
+            for o, ref in enumerate((own_ref, other_ref)):
+                d = 2 * x + o
+                block = ref[w * z.n_pair + x].astype(f32)
+                extra = block[lats : lats + SUBLANES]
+                leg_s[w, d * lats : (d + 1) * lats, :LANES] = block[:lats]
+                state_at = d * z.dev_rows
+                begin = lats + SUBLANES
+                state_s[w, state_at : state_at + z.dev_rows, :LANES] = block[begin : begin + z.dev_rows]
+                for q in range(z.groups):
+                    moved = extra if q == 0 else pltpu.roll(extra, LANES - q * z.unit, 1)
+                    at = q * SUBLANES
+                    if at < lats:
+                        leg_s[w, d * lats + at : d * lats + at + SUBLANES, LANES:] = moved
+                    else:
+                        at = at - lats
+                        count = min(SUBLANES, z.dev_rows - at)
+                        state_s[w, state_at + at : state_at + at + count, LANES:] = moved[:count]
+        if all_lats < leg_s.shape[1]:
+            leg_s[w, all_lats:, :] = jnp.zeros((leg_s.shape[1] - all_lats, wide), f32)
+
+    def legendre(w):
+        return leg_s[w].astype(bf)
+
+    def weighted(w):
+        table = leg_s[w]
+        column = table[:, z.used : z.used + 1] + table[:, z.used + 1 : z.used + 2]
+        return (table * column).astype(bf)
+
+    for w in range(z.n_wave):
+        state = state_s[w]
+        left = jnp.concatenate([state * member(w, j) for j in range(2 * slots)], 0).astype(bf)
+        out = matmul_nt(left, legendre(w))
+        for j in range(2 * slots):
+            fourier_s[pl.ds(w * 2 * slots + j, rows, stride=z.fine_columns), :] = out[j * rows : (j + 1) * rows]
+
+    both = 2 * z.fine_columns
+    for a in range(z.levels):
+        pieces = [
+            fourier_s[(a * z.nodes + b) * both : (a * z.nodes + b + 1) * both, :].astype(bf)
+            for b in range(z.nodes)
+        ]
+        grid = matmul(wave_ref[...], jnp.concatenate(pieces, 1))
+        product = (grid * grid).astype(bf)
+        back = matmul(quad_ref[a], product)
+        for b in range(z.nodes):
+            back_s[(a * z.nodes + b) * both : (a * z.nodes + b + 1) * both, :] = back[:, b * LANES : (b + 1) * LANES]
+
+    stacked = []
+    for w in range(z.n_wave):
+        left = jnp.concatenate(
+            [
+                back_s[pl.ds(w * 2 * slots + j, rows, stride=z.fine_columns), :].astype(bf)
+                for j in range(2 * slots)
+            ],
+            0,
+        )
+        out = matmul(left, weighted(w))
+        total = member(w, 0) * out[:rows]
+        for j in range(1, 2 * slots):
+            total = total + member(w, j) * out[j * rows : (j + 1) * rows]
+        tend_s[w, :rows, :] = total
+        stacked.append(state_s[w][:, :LANES] * keep(w))
+        stacked.append(total[:, :LANES] * keep(w))
+
+    modes = matmul_split(mix_to_ref[...], jnp.concatenate(stacked, 1))
+    evals, later, old_of, mid_of = [], [], [], []
+    for w in range(z.n_wave):
+        old, source = [], []
+        stiff = stiff_ref[w]
+        for b in range(z.nodes):
+            part = modes[b * per_node : (b + 1) * per_node]
+            old.append(part[:, 2 * w * LANES : (2 * w + 1) * LANES])
+            source.append(part[:, (2 * w + 1) * LANES : (2 * w + 2) * LANES] - stiff * old[-1])
+        divisor = 1.0 + STEP_HALF * stiff
+        mid = sum(quad_weights[0][b] * source[b] for b in range(z.nodes))
+        mid = (mid + old[0] + STEP_HALF * stiff * old[1]) / divisor
+        end = sum(quad_weights[1][b] * source[b] for b in range(z.nodes))
+        end = end + mid + STEP_HALF * stiff * old[2]
+        evals.append(old[1])
+        evals.append(mid)
+        later.append((end, divisor))
+        old_of.append(old)
+        mid_of.append(mid)
+
+    level_values = matmul_split(mix_from_ref[...], jnp.concatenate(evals, 1))
+    for w in range(z.n_wave):
+        left = jnp.concatenate(
+            [
+                level_values[:, (2 * w + e) * LANES : (2 * w + e + 1) * LANES] * slot(w, s)
+                for s in range(slots)
+                for e in range(2)
+            ],
+            0,
+        ).astype(bf)
+        out = matmul_nt(left, legendre(w)[:, :LANES])
+        for s in range(slots):
+            for e in range(2):
+                at = (s * 2 + e) * per_node
+                coarse_s[e, pl.ds(w * slots + s, per_node, stride=z.coarse_columns), :] = out[at : at + per_node]
+
+    both_c = 2 * z.coarse_columns
+    for a in range(z.levels):
+        pieces = [coarse_s[e, a * both_c : (a + 1) * both_c, :].astype(bf) for e in range(2)]
+        grid = matmul(coarse_wave_ref[...], jnp.concatenate(pieces, 1))
+        product = (grid * grid).astype(bf)
+        back = matmul(coarse_quad_ref[a], product)
+        for e in range(2):
+            coarse_back_s[e, a * both_c : (a + 1) * both_c, :] = back[:, e * LANES : (e + 1) * LANES]
+
+    tends = []
+    for w in range(z.n_wave):
+        left = jnp.concatenate(
+            [
+                coarse_back_s[e, pl.ds(w * slots + s, per_node, stride=z.coarse_columns), :].astype(bf)
+                for s in range(slots)
+                for e in range(2)
+            ],
+            0,
+        )
+        out = matmul(left, weighted(w)[:, :LANES])
+        for e in range(2):
+            total = None
+            for s in range(slots):
+                at = (s * 2 + e) * per_node
+                term = slot(w, s) * out[at : at + per_node]
+                total = term if total is None else total + term
+            tends.append(total)
+    coarse_modes = matmul_split(mix_back_ref[...], jnp.concatenate(tends, 1))
+    for w in range(z.n_wave):
+        before = coarse_modes[:, 2 * w * LANES : (2 * w + 1) * LANES]
+        fresh = coarse_modes[:, (2 * w + 1) * LANES : (2 * w + 2) * LANES]
+        end, divisor = later[w]
+        end = (end + STEP_HALF * (fresh - before)) / divisor
+        change_s[w, :per_node, :] = mid_of[w] - old_of[w][1]
+        change_s[w, per_node:, :] = end - old_of[w][2]
+
+    place = lax.axis_index("wave")
+    begin = pl.multiple_of(lax.div(lax.axis_index("lev"), 2) * (2 * z.dev_rows), SUBLANES)
+    mine = tend_s[place, pl.ds(begin, z.state_rows), :]
+    raised = matmul_split(lift_ref[...], change_s[place])
+    lane = lax.broadcasted_iota(jnp.int32, (z.state_rows, wide), 1)
+    for s in range(slots):
+        low = mine if s == 0 else pltpu.roll(mine, wide - s * z.coarse, 1)
+        high = pltpu.roll(mine, wide - (z.head + s * z.rest - z.coarse), 1)
+        values = jnp.where(lane < z.coarse, low, high)
+        for n in range(z.dev_rows):
+            a, b, c = n // (z.nodes * 2), n // 2 % z.nodes, n % 2
+            tend_ref[a, b, c, s : s + 1, :] = values[n : n + 1, : z.fine_rows]
+        low = raised if s == 0 else pltpu.roll(raised, LANES - s * z.coarse, 1)
+        low = jnp.where(lane[: low.shape[0], :LANES] < z.coarse, low, 0.0)
+        for n in range(low.shape[0]):
+            a, b, c = n // (2 * (z.nodes - 1)), n // 2 % (z.nodes - 1), n % 2
+            corrected_ref[a, b, c, s : s + 1, :] = (
+                state_ref[a, b + 1, c, s : s + 1, :] + low[n : n + 1, : z.fine_rows]
+            )
+
+
+def mix_constants(z):
+    level, node, part = np.arange(z.levels), np.arange(z.nodes), np.arange(2)
+
+    def pick(index):
+        return (np.asarray(index)[:, None] == level[None, :]).astype(np.float32)
+
+    def grid(*axes):
+        return [m.reshape(-1) for m in np.meshgrid(*axes, indexing="ij")]
+
+    def ordered(index, core):
+        lev, inner = index // z.lev_dev, index % z.lev_dev
+        return (lev ^ core) * z.lev_dev + inner
+
+    def thrice(matrix):
+        return np.concatenate([matrix] * 3, -1)
+
+    rb, rq, rc = grid(node, level, part)
+    ca, cb, cc = grid(level, node, part)
+    sa, sc = grid(level, part)
+    to_mask = (rb[:, None] == cb[None]) & (rc[:, None] == cc[None])
+    same_part = sc[:, None] == sc[None]
+    la, lb, lc = grid(np.arange(z.lev_dev), np.arange(z.nodes - 1), part)
+    kb, kq, kc = grid(np.arange(z.nodes - 1), level, part)
+    lift_mask = (lb[:, None] == kb[None]) & (lc[:, None] == kc[None])
+    by_core = range(2)
+    constants = (
+        pick(rq),
+        np.stack([thrice(pick(ordered(ca, k)).T) for k in by_core]),
+        thrice(to_mask),
+        np.stack([pick(ordered(sa, k)) for k in by_core]),
+        thrice(pick(sa).T),
+        thrice(same_part),
+        pick(sa),
+        np.stack([thrice(pick(ordered(sa, k)).T) for k in by_core]),
+        np.stack([pick(k * z.lev_dev + la) for k in range(z.n_lev)]),
+        thrice(pick(kq).T),
+        thrice(lift_mask),
+    )
+    return [jnp.asarray(c, jnp.float32) for c in constants]
+
+
+def replicated_plan(
+    fine_state, fold_pairs, legendre, gauss_weights, grid_coef, modes_from, modes_to, mode_rates
+):
+    z = Sizes(fine_state, legendre)
+    bf, f32 = jnp.bfloat16, jnp.float32
+    longitudes = grid_coef.shape[1]
+    vmem = pl.BlockSpec(memory_space=pltpu.VMEM)
+    smem = pl.BlockSpec(memory_space=pltpu.SMEM)
+    shape = jax.ShapeDtypeStruct
+    block = pl.pallas_call(
+        functools.partial(pack_kernel, z),
+        out_shape=shape((z.chips, z.block_rows, LANES), bf),
+        in_specs=[vmem] * 3,
+        out_specs=vmem,
+        scratch_shapes=[pltpu.VMEM((z.slots, z.state_rows, z.fine_rows), f32)],
+        name="pack",
+    )(fine_state, legendre, gauss_weights[None])
+    groups = [[2 * i + c for i in range(z.chips)] for c in range(2)]
+    own = lax.all_to_all(
+        block, ("wave", "lev"), 0, 0, tiled=True, axis_index_groups=groups
+    )
+    other = lax.ppermute(own, ("wave", "lev"), [(i, i ^ 1) for i in range(2 * z.chips)])
+
+    fine_amp, coarse_amp = z.fine_width**-0.5, z.coarse**-0.5
+    basis = wave_rows(z.fine_width, longitudes, fine_amp)
+    spread = interpolation(z.points, longitudes, 2 * (z.fine_width - 1))
+    spread *= 2.0 * z.fine_width / longitudes
+    coarse_spread = interpolation(z.coarse_points, longitudes, 2 * (z.coarse - 1))
+    coarse_spread *= 2.0 * z.coarse / (longitudes // 2) * (coarse_amp / fine_amp)
+    coarse_spread[1::2] = 0.0
+    sampled = wave_rows(z.fine_width, z.points, fine_amp).T
+    coarse_sampled = wave_rows(z.coarse, z.coarse_points, coarse_amp).T
+    constants = [jnp.asarray(c, bf) for c in (basis, spread, coarse_spread, sampled, coarse_sampled)]
+    mixes = mix_constants(z)
+    wide = 2 * LANES
+    n_lift = z.lev_dev * (z.nodes - 1) * 2
+    tables = pl.pallas_call(
+        functools.partial(tables_kernel, z),
+        out_shape=(
+            shape((z.points, 2 * z.fine_columns), bf),
+            shape((z.levels, 2 * z.fine_columns, z.points), bf),
+            shape((z.coarse_points, 2 * z.coarse_columns), bf),
+            shape((z.levels, 2 * z.coarse_columns, z.coarse_points), bf),
+            shape((z.rows, 3 * z.rows), bf),
+            shape((z.per_node, 3 * z.per_node), bf),
+            shape((z.per_node, 3 * z.per_node), bf),
+            shape((n_lift, 3 * (z.nodes - 1) * z.per_node), bf),
+            shape((z.fine_columns, wide), f32),
+            shape((z.coarse_columns, LANES), f32),
+            shape((z.n_wave, LANES), f32),
+            shape((z.n_wave, z.per_node, LANES), f32),
+        ),
+        in_specs=[smem, smem] + [vmem] * (4 + len(constants) + len(mixes)),
+        out_specs=(vmem,) * 12,
+        cost_estimate=pl.CostEstimate(flops=10**9, bytes_accessed=4 * 10**6, transcendentals=0),
+        name="tables",
+    )(mode_rates, fold_pairs, fold_pairs[None], grid_coef, modes_to, modes_from, *constants, *mixes)
+
+    lat_rows = round_up(z.n_lev * z.lats, LANES)
+    corrected, fine_tend = pl.pallas_call(
+        functools.partial(sweep_kernel, z),
+        out_shape=(
+            shape((z.lev_dev, z.nodes - 1, 2, z.slots, z.fine_rows), f32),
+            shape(fine_state.shape, f32),
+        ),
+        in_specs=[vmem] * 15,
+        out_specs=(vmem, vmem),
+        scratch_shapes=[
+            pltpu.VMEM((z.n_wave, lat_rows, wide), f32),
+            pltpu.VMEM((z.n_wave, z.rows, wide), f32),
+            pltpu.VMEM((z.rows * z.fine_columns, lat_rows), f32),
+            pltpu.VMEM((z.rows * z.fine_columns, lat_rows), f32),
+            pltpu.VMEM((z.n_wave, z.rows + SUBLANES, wide), f32),
+            pltpu.VMEM((2, z.per_node * z.coarse_columns, lat_rows), f32),
+            pltpu.VMEM((2, z.per_node * z.coarse_columns, lat_rows), f32),
+            pltpu.VMEM((z.n_wave, (z.nodes - 1) * z.per_node, LANES), f32),
+        ],
+        name="sweep",
+    )(own, other, fine_state, *tables)
+    return (corrected, fine_tend)
+
+
+def fits_replicated(fine_state, legendre):
+    n_wave, n_lev = lax.axis_size("wave"), lax.axis_size("lev")
+    if n_lev % 2 or fine_state.shape[1] != len(quad_weights[0]):
+        return False
+    z = Sizes(fine_state, legendre)
+    gathered = 32 * n_wave * n_lev * (legendre.size + fine_state.size)
+    return (
+        z.head <= LANES
+        and z.used > LANES
+        and z.used + 2 - LANES <= z.unit
+        and z.lats % SUBLANES == 0
+        and n_lev * z.lats <= LANES
+        and gathered <= REPLICATED_BYTES
+    )
+
+
+def per_device(fine_state, fold_pairs, legendre, *rest):
+    plan = replicated_plan if fits_replicated(fine_state, legendre) else split_plan
+    return plan(fine_state, fold_pairs, legendre, *rest)
+
+
 def solution(mesh):
     placed = (
         P("lev", None, None, "wave", None),

time: 131 us -> 41.4 us (0.32)
  blocking collectives: 59.5 us -> 17 us
  starting transfers between devices: 26.3 us -> 0.01 us
  waiting for transfers between devices: 22.5 us -> 0.01 us
  Pallas kernels: 0 us -> 18.6 us
  local copies, waits for them, and re-layouts: 12.5 us -> 4.68 us
  other arithmetic: 4.17 us -> 0 us
  matrix products: 3.8 us -> 0 us
    unnamed x4 -> x0, blocking collectives: 42.8 us -> none
    all_to_all x6 -> x0, starting transfers between devices: 26.3 us -> none  [the longest x2 9.25 us: coarse_eval(): lax.all_to_all(coarse_start(modes), 'wave', split_axis=5, concat_axis=3,...]
    all_to_all x6 -> x0, waiting for transfers between devices: 22.5 us -> none  [the longest x2 11.7 us: coarse_eval(): lax.all_to_all(coarse_grid_step(fourier), 'wave', split_axis=3, concat_ax...]
    pallas_call x0 -> x3, Pallas kernels: none -> 18.6 us  [the longest x1 9.73 us: replicated_plan(): pl.pallas_call(functools.partial(tables_kernel, z), out_shape=(shape((z.p...]
    all_to_all x0 -> x1, blocking collectives: none -> 17 us  [replicated_plan(): lax.all_to_all(block, ('wave', 'lev'), 0, 0, tiled=True, axis_index_group...]
    all_gather x3 -> x0, blocking collectives: 16.6 us -> none  [the longest x2 10.4 us: coarse_start(): gathered = lax.all_gather(modes, 'lev', axis=0, tiled=True)]
    unnamed x26 -> x5, local copies, waits for them, and re-layouts: 7.27 us -> 2.01 us
    dot_general x15 -> x0, matrix products: 3.8 us -> none  [the longest x3 1.55 us: grid_step(): jnp.einsum('abzk,cpmk->abcpmz', product, wave_table, preferred_element_ty...]
  transfers between devices with their start and end apart: 6 -> 1, of which waited for: 5 -> 0; matrix products, arithmetic and copies ran while one was open for 7% -> 0% of each run, Pallas kernels for 0% -> 24%
where the time goes in v2:
time: 41.4 us; the launch traced here: 40.9 us
  Pallas kernels  18.6 us (45%)
  blocking collectives  17 us (41%)
  local copies, waits for them, and re-layouts  4.68 us (11%)
  between operations  0.66 us (2%)
    all_to_all x1, blocking collectives, replicated_plan(): lax.all_to_all(block, ('wave', 'lev'), 0, 0, tiled=True, axis_index_group...  17 us
    pallas_call x1, Pallas kernels, replicated_plan(): pl.pallas_call(functools.partial(tables_kernel, z), out_shape=(shape((z.p...  9.73 us
    pallas_call x1, Pallas kernels, replicated_plan(): pl.pallas_call(functools.partial(sweep_kernel, z), out_shape=(shape((z.le...  7.26 us
    pallas_call x2, local copies, waits for them, and re-layouts, replicated_plan(): pl.pallas_call(functools.partial(sweep_kernel, z), out_shape=(shape((z.le...  2.67 us
    unnamed x5, local copies, waits for them, and re-layouts  2.01 us
    pallas_call x1, Pallas kernels, replicated_plan(): pl.pallas_call(functools.partial(pack_kernel, z), out_shape=shape((z.chip...  1.61 us
  transfers between devices with their start and end apart: 1, of which 0 were waited for; matrix products, arithmetic and copies ran while one was open for 0% of the time, Pallas kernels for 24%

profile of v2, /device:TPU:0, one launch (start us, length us, event | category | flops | bytes accessed | tf_op | source)
XLA Modules:
  0.0 40.9 jit_solution(16251626205238981380)
XLA Ops:
  0.6 1.3 %copy.26.state_ref = f32[2,3,2,3,49]{4,3,2,1,0:T(4,128)} copy(f32[2,3,2,3,49]{4,2,3,1,0:T(2,128)} %param.24) | data formatting | bytes 14112 | tf_op args[0]
  2.0 1.6 %pack.1 = bf16[16,48,128]{2,1,0:T(8,128)(2,1)} custom-call(f32[2,3,2,3,49]{4,3,2,1,0:T(4,128)} %copy.26.state_ref, bf16[3,24,49]{2,1,0:T(8,128)(2,1)} %leg_ref.1, f32[1,24]{1,0:T(1,128)} %bitcast.2), custom_call_target="tpu_custom_call" | custom-call | tf_op jit(solution)/shard_map/pack/pallas_call | solution.py:671
  3.6 17.0 %all_to_all.5.own_ref = bf16[16,48,128]{2,1,0:T(8,128)(2,1)S(1)} all-to-all(bf16[16,48,128]{2,1,0:T(8,128)(2,1)} %pack.1), channel_id=1, replica_groups={{0,2,4,6,8,10,12,14,16,18,20,22,24,26,28,30},{1,3,5,7,9,11,13,15,17,19,..., dimensions={0} | all-to-all | bytes 393216 | tf_op jit(solution)/shard_map/all_to_all | solution.py:680
  20.6 0.0 copy-start
  20.6 0.0 collective-permute-start
  20.6 9.7 %tables.1 = (bf16[192,96]{1,0:T(8,128)(2,1)}, bf16[8,96,192]{2,1,0:T(8,128)(2,1)}, bf16[96,48]{1,0:T(8,128)(2,1)}, bf16[8,48,96]{2,1,0:T(8,128)(2,1)}, bf16[48,1...) custom-call(f32[8]{0:T(128)} %rate_ref.1, ...), custom_call_target="tpu_custom_call" | custom-call | flops 1000000000 | bytes 4000000 | tf_op jit(solution)/shard_map/tables/pallas_call | solution.py:698
  30.3 0.0 copy-done
  30.3 0.0 collective-permute-done.other_ref
  30.3 0.0 copy-start.1
  30.3 0.7 %copy-done.1 = bf16[16,48,128]{2,1,0:T(8,128)(2,1)} copy-done((bf16[16,48,128]{2,1,0:T(8,128)(2,1)}, bf16[16,48,128]{2,1,0:T(8,128)(2,1)S(1)}, u32[]{:S(2)}) %copy-start.1) | copy-done | bytes 196632
  31.0 7.3 %sweep.1 = (f32[2,2,2,3,49]{4,3,2,1,0:T(4,128)}, f32[2,3,2,3,49]{4,3,2,1,0:T(4,128)}) custom-call(bf16[16,48,128]{2,1,0:T(8,128)(2,1)} %copy-done, bf16[16,48,128]{2,1,0:T(8,128)(2,1)} %copy-done.1, f32[2,3,2,3,49]{4,3,2,1,0:T(4,128)} %copy.26.state_ref, bf16[192,96]{1,0:T(8,128)(2,1)} %get-tuple-element.14.wave_ref, ...), custom_call_target="tpu_custom_call" | custom-call | tf_op jit(solution)/shard_map/sweep/pallas_call | solution.py:721
  38.3 1.3 %copy.28 = f32[2,2,2,3,49]{4,2,3,1,0:T(2,128)} copy(f32[2,2,2,3,49]{4,3,2,1,0:T(4,128)} %get-tuple-element.26) | data formatting | bytes 9408 | tf_op jit(solution)/shard_map/sweep/pallas_call | solution.py:721
  39.6 1.4 %copy.29 = f32[2,3,2,3,49]{4,2,3,1,0:T(2,128)} copy(f32[2,3,2,3,49]{4,3,2,1,0:T(4,128)} %get-tuple-element.27) | data formatting | bytes 14112 | tf_op jit(solution)/shard_map/sweep/pallas_call | solution.py:721
Async XLA Ops:
  20.6 9.7 %copy-start = (bf16[16,48,128]{2,1,0:T(8,128)(2,1)}, bf16[16,48,128]{2,1,0:T(8,128)(2,1)S(1)}, u32[]{:S(2)}) copy-start(bf16[16,48,128]{2,1,0:T(8,128)(2,1)S(1)} %all_to_all.5.own_ref) | copy-start | bytes 589828
  20.6 9.8 %collective-permute-start = (bf16[16,48,128]{2,1,0:T(8,128)(2,1)S(1)}, bf16[16,48,128]{2,1,0:T(8,128)(2,1)S(1)}, u32[]{:S(2)}, u32[]{:S(2)}) collective-permute-start(bf16[16,48,128]{2,1,0:T(8,128)(2,1)S(1)} %all_to_all.5.own_ref), channel_id=1, source_target_pairs={{0,1},{1,0},{2,3},{3,2},{4,5},{5,4},{6,7},{7,6},{8,9},{9,8},{10,11... | collective-permute-start | bytes 589832 | tf_op jit(solution)/shard_map/ppermute | solution.py:683
  30.3 0.7 %copy-start.1 = (bf16[16,48,128]{2,1,0:T(8,128)(2,1)}, bf16[16,48,128]{2,1,0:T(8,128)(2,1)S(1)}, u32[]{:S(2)}) copy-start(bf16[16,48,128]{2,1,0:T(8,128)(2,1)S(1)} %collective-permute-done.other_ref) | copy-start | bytes 589828
